TPU v7x, 256 devices: a whole 4x4x8 slice. The times are simulated.
256 devices in a mesh: group: 8 (over z_lo, y), dev: 32 (over z_hi, x, core).
Axes of the slice: x: 4, y: 4, z: 8 (z_hi: 4, z_lo: 2; z = z_hi * 2 + z_lo), core: 2. Of those that a mesh axis runs over, the one named last changes fastest.
Arguments:
- right_side: float32 [3, 16, 64, 64, 128], P(None, 'group', 'dev'), may hold values from -60 to 60
- stiff_diag: float32 [3, 3, 16, 4096], P(None, None, 'group', 'dev'), may hold values from -0.1 to 12.75, as said below
- stiff_lower: float32 [3, 3, 13, 16, 4096], P(None, None, None, 'group', 'dev'), may hold values from -0.08 to 0.08
- fsai_diag: float32 [3, 3, 16, 4096], P(None, None, 'group', 'dev'), may hold values from -0.1 to 1, as said below
- fsai_lower: float32 [3, 3, 13, 16, 4096], P(None, None, None, 'group', 'dev'), may hold values from -0.12 to 0.12
- fsai_pattern: int32 [13, 16, 4096], P(None, 'group', 'dev'), may hold values 0 or 1
Outputs:
- solution: float32 [3, 16, 64, 64, 128], P(None, 'group', 'dev')
- residual: float32 [3, 16, 64, 64, 128], P(None, 'group', 'dev')
Inputs may be any that keep to these rules, and one draw needn't show every extreme that they name: `stiff_diag`: each 3 by 3 block is symmetric. `fsai_diag`: each 3 by 3 block is zero above its diagonal and positive on it.
All inputs are finite; a program needn't handle non-finite values. No bound on the sum of `fsai_pattern` on one device may be relied on, other than what follows from the above.
Results may differ from a plain program's by a relative error of at most 0.0003.
Values sent between devices are 32-bit elements; how exact they have to be, the bound alone decides.
A program may use at most 128 MiB of HBM per device.

v0:
```python
import jax
import jax.numpy as jnp
from jax import lax
from jax.sharding import PartitionSpec as P

ITERS = 2


highest = lax.Precision.HIGHEST
lower_offsets = [(0, 0, -1), (0, -1, -1), (0, -1, 0), (0, -1, 1)] + [
    (-1, row_step, column_step) for row_step in (-1, 0, 1) for column_step in (-1, 0, 1)
]


def with_halo(block, sides, width):
    for axis, dim in sides:
        count = lax.axis_size(axis)
        forward = [(i, i + 1) for i in range(count - 1)]
        backward = [(target, source) for source, target in forward]
        low = lax.ppermute(
            lax.slice_in_dim(block, block.shape[dim] - width, None, axis=dim), axis, forward
        )
        high = lax.ppermute(lax.slice_in_dim(block, 0, width, axis=dim), axis, backward)
        block = jnp.concatenate([low, block, high], axis=dim)
    return block


def from_behind(value, axis, steps):
    count = lax.axis_size(axis)
    first, last = (max(0, -steps), min(count, count - steps))
    return lax.ppermute(value, axis, [(source, source + steps) for source in range(first, last)])


def block_mul(coeffs, vector):
    return jnp.stack(
        [
            coeffs[target, 0][..., None] * vector[0]
            + coeffs[target, 1][..., None] * vector[1]
            + coeffs[target, 2][..., None] * vector[2]
            for target in range(3)
        ]
    )


def block_mul_transposed(coeffs, vector):
    return jnp.stack(
        [
            coeffs[0, target][..., None] * vector[0]
            + coeffs[1, target][..., None] * vector[1]
            + coeffs[2, target][..., None] * vector[2]
            for target in range(3)
        ]
    )


def pad_columns(vector):
    return jnp.pad(vector, ((0, 0), (0, 0), (0, 0), (1, 1), (0, 0)))


def local_gram(left_block, right_block):
    return jnp.einsum("azxyr,azxys->rs", left_block, right_block, precision=highest)


def combine(vector, coeffs):
    return jnp.einsum("azxyr,rs->azxys", vector, coeffs, precision=highest)


def gram_solve(matrix, right_terms):
    factor = jnp.linalg.cholesky(matrix)
    halfway = lax.linalg.triangular_solve(factor, right_terms, left_side=True, lower=True)
    return lax.linalg.triangular_solve(
        factor, halfway, left_side=True, lower=True, transpose_a=True
    )


def per_device(right_side, stiff_diag, stiff_lower, fsai_diag, fsai_lower, fsai_pattern):
    local_planes = right_side.shape[1]
    local_rows = right_side.shape[2]
    line_length = right_side.shape[3]
    slot_count = stiff_lower.shape[2]
    stiff_d = stiff_diag.reshape(3, 3, local_planes, local_rows, line_length)
    fsai_d = fsai_diag.reshape(3, 3, local_planes, local_rows, line_length)
    stiff_low = stiff_lower.reshape(3, 3, slot_count, local_planes, local_rows, line_length)
    kept = fsai_pattern.astype(jnp.float32)
    fsai_low = (fsai_lower * kept[None, None]).reshape(
        3, 3, slot_count, local_planes, local_rows, line_length
    )

    def lower_window(vector):
        rimmed = with_halo(vector, (("dev", 2),), 1)
        plane_under = from_behind(rimmed[:, local_planes - 1 :], "group", 1)
        return pad_columns(jnp.concatenate([plane_under, rimmed], axis=1))

    def gather_lower(diag_blocks, low_blocks, window_data, vector):
        result = block_mul(diag_blocks, vector)
        for slot_index, (depth_step, row_step, column_step) in enumerate(lower_offsets):
            picked = window_data[
                :,
                1 + depth_step : 1 + depth_step + local_planes,
                1 + row_step : 1 + row_step + local_rows,
                1 + column_step : 1 + column_step + line_length,
            ]
            result = result + block_mul(low_blocks[:, :, slot_index], picked)
        return result

    def push_upper(low_blocks, vector):
        buffer = None
        for slot_index, (depth_step, row_step, column_step) in enumerate(lower_offsets):
            slot_term = block_mul_transposed(low_blocks[:, :, slot_index], vector)
            placed = jnp.pad(
                slot_term,
                (
                    (0, 0),
                    (1 + depth_step, -depth_step),
                    (1 + row_step, 1 - row_step),
                    (1 + column_step, 1 - column_step),
                    (0, 0),
                ),
            )
            buffer = placed if buffer is None else buffer + placed
        inner_part = buffer[:, :, :, 1 : line_length + 1]
        rim_rows = jnp.concatenate(
            [inner_part[:, :, :1], inner_part[:, :, local_rows + 1 :]], axis=2
        )
        arrived = with_halo(rim_rows, (("dev", 2),), 1)
        core_part = inner_part[:, :, 1 : local_rows + 1]
        core_part = core_part.at[:, :, :1].add(arrived[:, :, :1])
        core_part = core_part.at[:, :, local_rows - 1 :].add(arrived[:, :, 3:])
        returned = from_behind(core_part[:, :1], "group", -1)
        return core_part[:, 1:].at[:, local_planes - 1 :].add(returned)

    def apply_fsai(vector):
        return gather_lower(fsai_d, fsai_low, lower_window(vector), vector)

    def apply_fsai_transposed(vector):
        diagonal_part = block_mul_transposed(fsai_d, vector)
        upper_sum = push_upper(fsai_low, vector)
        return diagonal_part + upper_sum

    def residual_sum(weighted):
        return lax.psum(local_gram(weighted, weighted), ("group", "dev"))

    solution = jnp.zeros_like(right_side)
    residual = right_side
    weighted = apply_fsai(residual)
    resid_gram = residual_sum(weighted)
    direction = apply_fsai_transposed(weighted)
    for iteration in range(ITERS):
        lower_sum = gather_lower(stiff_d, stiff_low, lower_window(direction), direction)
        apply_upper_sum = push_upper(stiff_low, direction)
        product = lower_sum + apply_upper_sum
        step_size = gram_solve(
            lax.psum(local_gram(direction, product), ("group", "dev")), resid_gram
        )
        solution = solution + combine(direction, step_size)
        residual = residual - combine(product, step_size)
        if iteration + 1 < ITERS:
            weighted = apply_fsai(residual)
            next_gram = residual_sum(weighted)
            precond = apply_fsai_transposed(weighted)
            conjugacy = gram_solve(resid_gram, next_gram)
            direction = precond + combine(direction, conjugacy)
            resid_gram = next_gram
    return (solution, residual)


def solution(mesh):
    return jax.shard_map(
        per_device,
        mesh=mesh,
        in_specs=(
            P(None, "group", "dev", None, None),
            P(None, None, "group", "dev"),
            P(None, None, None, "group", "dev"),
            P(None, None, "group", "dev"),
            P(None, None, None, "group", "dev"),
            P(None, "group", "dev"),
        ),
        out_specs=(P(None, "group", "dev", None, None), P(None, "group", "dev", None, None)),
        check_vma=False,
    )
```

profile of v0, /device:TPU:1, one launch (start us, length us, event | category | flops | bytes accessed | tf_op | source)
XLA Modules:
  0.0 1072.1 jit_solution(4820610917557618189)
XLA Ops:
  8.3 4.5 collective-permute-start
  12.8 1.9 collective-permute-start.1
  25.8 3.4 collective-permute-start.2
  31.0 5.5 collective-permute-done.2
  63.6 1.4 fusion.48
  65.1 4.8 collective-permute-start.3
  71.4 1.9 collective-permute-start.4
  74.1 5.4 collective-permute-done.4
  81.5 1.4 convolution_bitcast_fusion.5
  83.0 3.7 collective-permute-done.5
  87.0 3.9 collective-permute-start.6
  90.9 2.3 collective-permute-start.7
  102.9 1.4 fusion.36
  104.4 3.6 collective-permute-start.9
  108.1 1.9 collective-permute-start.10
  110.0 3.9 collective-permute-start.8
  114.5 1.6 collective-permute-done.10
  117.5 4.0 collective-permute-done.8
  127.1 1.4 convolution_bitcast_fusion.6
  128.8 264.0 %all-reduce.65.cloned.1.call-done = (f32[128,128]{0,1:T(8,128)}, f32[128,128]{0,1:T(8,128)}) async-done(((f32[128,128]{0,1:T(8,128)}, f32[128,128]{0,1:T(8,128)}), (f32[128,128]{0,1:T(8,128)}, f32[128,128]{0,1:T(8,128)})) %all-reduce.65.cloned.1.call-update) | async-done | bytes 131088 | tf_op jit(solution)/shard_map/psum | solution.py:141
  394.7 11.7 %cholesky.59 = f32[128,128]{1,0:T(8,128)S(1)} custom-call(f32[128,128]{1,0:T(8,128)S(1)} %fusion.164), custom_call_target="Cholesky" | custom-call | tf_op jit(solution)/shard_map/jit(cholesky)/cholesky | solution.py:69
  407.7 9.8 custom-call.13
  420.4 4.9 collective-permute-start.12
  425.3 1.9 collective-permute-start.13
  427.3 11.7 %cholesky.70 = f32[128,128]{1,0:T(8,128)S(1)} custom-call(f32[128,128]{1,0:T(8,128)S(1)} %fusion.160), custom_call_target="Cholesky" | custom-call | tf_op jit(solution)/shard_map/jit(cholesky)/cholesky | solution.py:69
  440.7 1.6 collective-permute-start.14
  444.3 6.6 collective-permute-done.14
  477.9 1.4 fusion.24
  480.2 3.6 collective-permute-start.15
  484.4 10.4 custom-call.15
  494.9 1.9 collective-permute-start.16
  496.8 1.4 convolution_bitcast_fusion.3
  499.4 3.8 collective-permute-done.16
  504.3 1.3 collective-permute-start.17
  505.6 238.5 %all-reduce.61.cloned.1.call-done = f32[128,128]{1,0:T(8,128)} async-done(((f32[128,128]{1,0:T(8,128)}), f32[128,128]{1,0:T(8,128)}) %all-reduce.61.cloned.1.call-update) | async-done | bytes 65552 | tf_op jit(solution)/shard_map/psum | solution.py:141
  757.1 2.5 collective-permute-start.18
  759.6 1.9 collective-permute-start.19
  763.2 1.4 fusion.12
  764.7 4.4 collective-permute-start.21
  769.1 1.9 collective-permute-start.22
  771.0 2.7 collective-permute-start.20
  774.2 2.9 collective-permute-done.22
  777.2 1.5 collective-permute-start.23
  778.7 1.8 collective-permute-done.20
  786.3 1.4 convolution_bitcast_fusion.1
  787.8 249.6 %all-reduce.63.cloned.1.call-done = f32[128,128]{0,1:T(8,128)} async-done(((f32[128,128]{0,1:T(8,128)}), f32[128,128]{0,1:T(8,128)}) %all-reduce.63.cloned.1.call-update) | async-done | bytes 65552 | tf_op jit(solution)/shard_map/psum | solution.py:153
  1039.1 11.7 %cholesky.81 = f32[128,128]{1,0:T(8,128)S(1)} custom-call(f32[128,128]{1,0:T(8,128)S(1)} %fusion.156), custom_call_target="Cholesky" | custom-call | tf_op jit(solution)/shard_map/jit(cholesky)/cholesky | solution.py:69
  1052.2 9.8 custom-call.17
  (785 shorter events, 125.9 us)
Async XLA Ops:
  7.2 385.7 %all-reduce.65.cloned.1.call-start = ((), (), s32[]{:S(2)}) async-start(), calls=%async_computation.2 | async-start | bytes 262144 | tf_op jit(solution)/shard_map/psum | solution.py:141
  8.3 17.4 %collective-permute-start = (f32[3,2,1,64,128]{4,3,2,1,0:T(8,128)S(1)}, f32[3,2,1,64,128]{4,3,2,1,0:T(8,128)S(1)}, u32[]{:S(2)}, u32[]{:S(2)}) collective-permute-start(f32[3,2,1,64,128]{4,3,2,1,0:T(8,128)S(1)} %get-tuple-element.502), channel_id=1, source_target_pairs={{0,1},{1,2},{2,3},{3,4},{4,5},{5,6},{6,7},{7,8},{8,9},{9,10},{10,1... | collective-permute-start | bytes 589832 | tf_op jit(solution)/shard_map/ppermute | solution.py:20
  12.8 13.0 %collective-permute-start.1 = (f32[3,2,1,64,128]{4,3,2,1,0:T(8,128)S(1)}, f32[3,2,1,64,128]{4,3,2,1,0:T(8,128)S(1)}, u32[]{:S(2)}, u32[]{:S(2)}) collective-permute-start(f32[3,2,1,64,128]{4,3,2,1,0:T(8,128)S(1)} %get-tuple-element.501), channel_id=1, source_target_pairs={{1,0},{2,1},{3,2},{4,3},{5,4},{6,5},{7,6},{8,7},{9,8},{10,9},{11,1... | collective-permute-start | bytes 589832 | tf_op jit(solution)/shard_map/ppermute | solution.py:23
  18.4 103.2 %copy-start.17 = (f32[2,2,64]{2,1,0:T(2,128)}, f32[2,2,64]{2,1,0:T(2,128)S(1)}, u32[]{:S(2)}) copy-start(f32[2,2,64]{2,1,0:T(2,128)S(1)} %get-tuple-element.651) | copy-start | bytes 3076
  18.4 103.2 %copy-start.19 = (f32[2,2,64]{2,1,0:T(2,128)}, f32[2,2,64]{2,1,0:T(2,128)S(1)}, u32[]{:S(2)}) copy-start(f32[2,2,64]{2,1,0:T(2,128)S(1)} %get-tuple-element.658) | copy-start | bytes 3076
  18.4 103.2 %copy-start.21 = (f32[2,2,64]{2,1,0:T(2,128)}, f32[2,2,64]{2,1,0:T(2,128)S(1)}, u32[]{:S(2)}) copy-start(f32[2,2,64]{2,1,0:T(2,128)S(1)} %get-tuple-element.659) | copy-start | bytes 3076
  18.4 103.7 %copy-start.11 = (f32[2,2,64]{2,1,0:T(2,128)}, f32[2,2,64]{2,1,0:T(2,128)S(1)}, u32[]{:S(2)}) copy-start(f32[2,2,64]{2,1,0:T(2,128)S(1)} %get-tuple-element.655) | copy-start | bytes 3076
  18.4 103.7 %copy-start.13 = (f32[2,2,64]{2,1,0:T(2,128)}, f32[2,2,64]{2,1,0:T(2,128)S(1)}, u32[]{:S(2)}) copy-start(f32[2,2,64]{2,1,0:T(2,128)S(1)} %get-tuple-element.656) | copy-start | bytes 3076
  18.5 103.7 %copy-start.15 = (f32[2,2,64]{2,1,0:T(2,128)}, f32[2,2,64]{2,1,0:T(2,128)S(1)}, u32[]{:S(2)}) copy-start(f32[2,2,64]{2,1,0:T(2,128)S(1)} %get-tuple-element.657) | copy-start | bytes 3076
  18.5 104.2 %copy-start.5 = (f32[2,2,64]{2,1,0:T(2,128)}, f32[2,2,64]{2,1,0:T(2,128)S(1)}, u32[]{:S(2)}) copy-start(f32[2,2,64]{2,1,0:T(2,128)S(1)} %get-tuple-element.652) | copy-start | bytes 3076
  18.5 104.2 %copy-start.7 = (f32[2,2,64]{2,1,0:T(2,128)}, f32[2,2,64]{2,1,0:T(2,128)S(1)}, u32[]{:S(2)}) copy-start(f32[2,2,64]{2,1,0:T(2,128)S(1)} %get-tuple-element.653) | copy-start | bytes 3076
  18.5 104.2 %copy-start.9 = (f32[2,2,64]{2,1,0:T(2,128)}, f32[2,2,64]{2,1,0:T(2,128)S(1)}, u32[]{:S(2)}) copy-start(f32[2,2,64]{2,1,0:T(2,128)S(1)} %get-tuple-element.654) | copy-start | bytes 3076
  23.2 102.4 %copy-start.25 = (f32[2,2,64]{2,1,0:T(2,128)}, f32[2,2,64]{2,1,0:T(2,128)S(1)}, u32[]{:S(2)}) copy-start(f32[2,2,64]{2,1,0:T(2,128)S(1)} %get-tuple-element.637) | copy-start | bytes 3076
  23.2 102.4 %copy-start.27 = (f32[2,2,64]{2,1,0:T(2,128)}, f32[2,2,64]{2,1,0:T(2,128)S(1)}, u32[]{:S(2)}) copy-start(f32[2,2,64]{2,1,0:T(2,128)S(1)} %get-tuple-element.638) | copy-start | bytes 3076
  23.2 102.4 %copy-start.29 = (f32[2,2,64]{2,1,0:T(2,128)}, f32[2,2,64]{2,1,0:T(2,128)S(1)}, u32[]{:S(2)}) copy-start(f32[2,2,64]{2,1,0:T(2,128)S(1)} %get-tuple-element.639) | copy-start | bytes 3076
  23.2 102.4 %copy-start.31 = (f32[2,2,64]{2,1,0:T(2,128)}, f32[2,2,64]{2,1,0:T(2,128)S(1)}, u32[]{:S(2)}) copy-start(f32[2,2,64]{2,1,0:T(2,128)S(1)} %get-tuple-element.640) | copy-start | bytes 3076
  23.2 102.4 %copy-start.33 = (f32[2,2,64]{2,1,0:T(2,128)}, f32[2,2,64]{2,1,0:T(2,128)S(1)}, u32[]{:S(2)}) copy-start(f32[2,2,64]{2,1,0:T(2,128)S(1)} %get-tuple-element.641) | copy-start | bytes 3076
  23.2 102.4 %copy-start.35 = (f32[2,2,64]{2,1,0:T(2,128)}, f32[2,2,64]{2,1,0:T(2,128)S(1)}, u32[]{:S(2)}) copy-start(f32[2,2,64]{2,1,0:T(2,128)S(1)} %get-tuple-element.851) | copy-start | bytes 3076
  23.2 102.4 %copy-start.37 = (f32[2,2,64]{2,1,0:T(2,128)}, f32[2,2,64]{2,1,0:T(2,128)S(1)}, u32[]{:S(2)}) copy-start(f32[2,2,64]{2,1,0:T(2,128)S(1)} %get-tuple-element.852) | copy-start | bytes 3076
  23.2 102.4 %copy-start.39 = (f32[2,2,64]{2,1,0:T(2,128)}, f32[2,2,64]{2,1,0:T(2,128)S(1)}, u32[]{:S(2)}) copy-start(f32[2,2,64]{2,1,0:T(2,128)S(1)} %get-tuple-element.853) | copy-start | bytes 3076
  23.2 102.4 %copy-start.41 = (f32[2,2,64]{2,1,0:T(2,128)}, f32[2,2,64]{2,1,0:T(2,128)S(1)}, u32[]{:S(2)}) copy-start(f32[2,2,64]{2,1,0:T(2,128)S(1)} %get-tuple-element.854) | copy-start | bytes 3076
  23.3 102.4 %copy-start.43 = (f32[2,2,64]{2,1,0:T(2,128)}, f32[2,2,64]{2,1,0:T(2,128)S(1)}, u32[]{:S(2)}) copy-start(f32[2,2,64]{2,1,0:T(2,128)S(1)} %get-tuple-element.855) | copy-start | bytes 3076
  25.8 10.7 collective-permute-start.2
  65.1 8.9 collective-permute-start.3
  71.4 8.0 collective-permute-start.4
  79.6 7.2 collective-permute-start.5
  87.0 14.9 %collective-permute-start.6 = (f32[3,2,1,64,128]{4,3,2,1,0:T(8,128)S(1)}, f32[3,2,1,64,128]{4,3,2,1,0:T(8,128)S(1)}, u32[]{:S(2)}, u32[]{:S(2)}) collective-permute-start(f32[3,2,1,64,128]{4,3,2,1,0:T(8,128)S(1)} %get-tuple-element.416), channel_id=1, source_target_pairs={{0,1},{1,2},{2,3},{3,4},{4,5},{5,6},{6,7},{7,8},{8,9},{9,10},{10,1... | collective-permute-start | bytes 589832 | tf_op jit(solution)/shard_map/ppermute | solution.py:20
  90.9 19.0 %collective-permute-start.7 = (f32[3,2,1,64,128]{4,3,2,1,0:T(8,128)S(1)}, f32[3,2,1,64,128]{4,3,2,1,0:T(8,128)S(1)}, u32[]{:S(2)}, u32[]{:S(2)}) collective-permute-start(f32[3,2,1,64,128]{4,3,2,1,0:T(8,128)S(1)} %get-tuple-element.417), channel_id=1, source_target_pairs={{1,0},{2,1},{3,2},{4,3},{5,4},{6,5},{7,6},{8,7},{9,8},{10,9},{11,1... | collective-permute-start | bytes 589832 | tf_op jit(solution)/shard_map/ppermute | solution.py:23
  104.4 10.0 collective-permute-start.9
  108.1 8.0 collective-permute-start.10
  110.0 11.5 %collective-permute-start.8 = (f32[3,1,4,64,128]{4,3,2,1,0:T(8,128)S(1)}, f32[3,1,4,64,128]{4,3,2,1,0:T(8,128)S(1)}, u32[]{:S(2)}, u32[]{:S(2)}) collective-permute-start(f32[3,1,4,64,128]{4,3,2,1,0:T(8,128)S(1)} %pad_maximum_fusion.5), channel_id=1, source_target_pairs={{0,32},{32,64},{64,96},{96,128},{128,160},{160,192},{192,224},{1,3... | collective-permute-start | bytes 1179656 | tf_op jit(solution)/shard_map/ppermute | solution.py:31
  116.2 10.2 collective-permute-start.11
  128.6 615.4 %all-reduce.61.cloned.1.call-start = ((), (), s32[]{:S(2)}) async-start(), calls=%async_computation | async-start | bytes 131072 | tf_op jit(solution)/shard_map/psum | solution.py:141
  420.4 20.2 %collective-permute-start.12 = (f32[3,2,1,64,128]{4,3,2,1,0:T(8,128)S(1)}, f32[3,2,1,64,128]{4,3,2,1,0:T(8,128)S(1)}, u32[]{:S(2)}, u32[]{:S(2)}) collective-permute-start(f32[3,2,1,64,128]{4,3,2,1,0:T(8,128)S(1)} %get-tuple-element.410), channel_id=1, source_target_pairs={{0,1},{1,2},{2,3},{3,4},{4,5},{5,6},{6,7},{7,8},{8,9},{9,10},{10,1... | collective-permute-start | bytes 589832 | tf_op jit(solution)/shard_map/ppermute | solution.py:20
  425.3 15.3 %collective-permute-start.13 = (f32[3,2,1,64,128]{4,3,2,1,0:T(8,128)S(1)}, f32[3,2,1,64,128]{4,3,2,1,0:T(8,128)S(1)}, u32[]{:S(2)}, u32[]{:S(2)}) collective-permute-start(f32[3,2,1,64,128]{4,3,2,1,0:T(8,128)S(1)} %get-tuple-element.411), channel_id=1, source_target_pairs={{1,0},{2,1},{3,2},{4,3},{5,4},{6,5},{7,6},{8,7},{9,8},{10,9},{11,1... | collective-permute-start | bytes 589832 | tf_op jit(solution)/shard_map/ppermute | solution.py:23
  440.7 10.2 collective-permute-start.14
  480.2 18.1 %collective-permute-start.15 = (f32[3,3,1,64,128]{4,3,2,1,0:T(8,128)}, f32[3,3,1,64,128]{4,3,2,1,0:T(8,128)}, u32[]{:S(2)}, u32[]{:S(2)}) collective-permute-start(f32[3,3,1,64,128]{4,3,2,1,0:T(8,128)} %get-tuple-element.166), channel_id=1, source_target_pairs={{0,1},{1,2},{2,3},{3,4},{4,5},{5,6},{6,7},{7,8},{8,9},{9,10},{10,1... | collective-permute-start | bytes 884744 | tf_op jit(solution)/shard_map/ppermute | solution.py:20
  494.9 8.3 collective-permute-start.16
  498.3 245.8 %copy-start.3 = (f32[1,128,128]{1,2,0:T(8,128)S(1)}, f32[1,128,128]{1,2,0:T(8,128)}, u32[]{:S(2)}) copy-start(f32[1,128,128]{1,2,0:T(8,128)} %custom-call.15) | copy-start | bytes 196612
  498.3 539.0 %all-reduce.63.cloned.1.call-start = ((), (), s32[]{:S(2)}) async-start(), calls=%async_computation.1 | async-start | bytes 131072 | tf_op jit(solution)/shard_map/psum | solution.py:153
  504.3 241.2 %collective-permute-start.17 = (f32[3,1,2,64,128]{4,3,2,1,0:T(8,128)S(1)}, f32[3,1,2,64,128]{4,3,2,1,0:T(8,128)S(1)}, u32[]{:S(2)}, u32[]{:S(2)}) collective-permute-start(f32[3,1,2,64,128]{4,3,2,1,0:T(8,128)S(1)} %slice.4621), channel_id=1, source_target_pairs={{32,0},{64,32},{96,64},{128,96},{160,128},{192,160},{224,192},{33,... | collective-permute-start | bytes 589832 | tf_op jit(solution)/shard_map/ppermute | solution.py:31
  757.1 5.1 collective-permute-start.18
  759.6 11.4 %collective-permute-start.19 = (f32[3,2,1,64,128]{4,3,2,1,0:T(8,128)S(1)}, f32[3,2,1,64,128]{4,3,2,1,0:T(8,128)S(1)}, u32[]{:S(2)}, u32[]{:S(2)}) collective-permute-start(f32[3,2,1,64,128]{4,3,2,1,0:T(8,128)S(1)} %get-tuple-element.325), channel_id=1, source_target_pairs={{1,0},{2,1},{3,2},{4,3},{5,4},{6,5},{7,6},{8,7},{9,8},{10,9},{11,1... | collective-permute-start | bytes 589832 | tf_op jit(solution)/shard_map/ppermute | solution.py:23
  764.7 9.5 collective-permute-start.21
  769.1 8.0 collective-permute-start.22
  771.0 9.5 collective-permute-start.20
  777.2 8.3 collective-permute-start.23
  786.3 275.7 %copy-start.2 = (f32[128,128]{1,0:T(8,128)S(1)}, f32[128,128]{1,0:T(8,128)}, u32[]{:S(2)}) copy-start(f32[128,128]{1,0:T(8,128)} %all-reduce.61.cloned.1.call-done) | copy-start | bytes 196612
  (259 other events, 2397.2 us)
Sparse Core Ops, SparseCore 0:
  128.7 264.0 all-reduce.64
  498.4 245.5 all-reduce.60
  787.9 249.4 all-reduce.62
where the time goes:
time: 1080 us; the launch traced here: 1070 us
  waiting for transfers between devices  788 us (73%)
  other arithmetic  168 us (16%)
  starting transfers between devices  65.3 us (6%)
  between operations  19.7 us (2%)
  local copies, waits for them, and re-layouts  17.9 us (2%)
  matrix products  12.7 us (1%)
    psum x2, waiting for transfers between devices, residual_sum(): return lax.psum(local_gram(weighted, weighted), ('group', 'dev'))  503 us
    psum x1, waiting for transfers between devices, per_device(): lax.psum(local_gram(direction, product), ('group', 'dev'))  250 us
    add x55, other arithmetic, block_mul(): coeffs[target, 0][..., None] * vector[0]  42.9 us
    add x50, other arithmetic, block_mul_transposed(): coeffs[0, target][..., None] * vector[0]  41.6 us
    another operation x9, other arithmetic, gram_solve(): factor = jnp.linalg.cholesky(matrix)  37.2 us
    ppermute x8, starting transfers between devices, with_halo(): lax.ppermute(lax.slice_in_dim(block, block.shape[dim] - width, None, axis...  32.3 us
    another operation x6, other arithmetic, gram_solve(): lax.linalg.triangular_solve(factor, halfway, left_side=True, lower=True,...  32 us
    ppermute x8, waiting for transfers between devices, from_behind(): lax.ppermute(value, axis, [(source, source + steps) for source in range(f...  21.7 us
  transfers between devices with their start and end apart: 27, of which 13 were waited for; matrix products, arithmetic and copies ran while one was open for 7% of the time, Pallas kernels for 0%

commit v1 on v0

v1 whole, which is shorter than its diff:
```python
import functools

import jax
import jax.numpy as jnp
from jax import lax
from jax.experimental import pallas as pl
from jax.experimental.pallas import tpu as pltpu
from jax.sharding import PartitionSpec as P

MESH = pl.DeviceIdType.MESH
highest = lax.Precision.HIGHEST
GROUP_Y = 4
DEV_XC = 8
PLANE_PEERS = GROUP_Y * DEV_XC
lower_offsets = [(0, 0, -1), (0, -1, -1), (0, -1, 0), (0, -1, 1)] + [
    (-1, row_step, column_step) for row_step in (-1, 0, 1) for column_step in (-1, 0, 1)
]


def mm(left, right, dims=((1,), (0,))):
    return lax.dot_general(left, right, (dims, ((), ())), precision=highest, preferred_element_type=jnp.float32)


def invert(*matrices):
    size = matrices[0].shape[0]
    lane = lax.broadcasted_iota(jnp.int32, (size, size), 1)
    sub = lax.broadcasted_iota(jnp.int32, (size, size), 0)
    lane_row = lax.broadcasted_iota(jnp.int32, (1, size), 1)
    matrices = list(matrices)
    for k in range(size):
        for i, m in enumerate(matrices):
            inverse = 1.0 / m[k : k + 1, k : k + 1]
            row = jnp.where(lane_row == k, inverse, m[k : k + 1, :] * inverse)
            column = m[:, k : k + 1]
            swept = jnp.where(lane == k, 0.0, m) - column * row
            matrices[i] = jnp.where(sub == k, jnp.broadcast_to(row, m.shape), swept)
    return matrices


def finish_kernel(grams_ref, right_ref, basis_ref, solution_ref, residual_ref):
    size = grams_ref.shape[1]
    resid, energy, coupling, outer = [grams_ref[i * size : (i + 1) * size, :] for i in range(4)]
    identity = (
        lax.broadcasted_iota(jnp.int32, (size, size), 0) == lax.broadcasted_iota(jnp.int32, (size, size), 1)
    ).astype(jnp.float32)
    trans = ((0,), (0,))
    energy = 0.5 * (energy + energy.T)
    energy_inv, resid_inv = invert(energy, resid)
    step = mm(energy_inv, resid)
    shift = mm(energy, step)
    next_gram = resid - shift - shift.T + mm(step, mm(coupling, step), trans)
    grow = identity + mm(resid_inv, next_gram)
    cross = mm(grow, mm(coupling, step), trans)
    next_energy = mm(grow, mm(energy, grow), trans) - cross - cross.T + mm(step, mm(outer, step), trans)
    next_energy = 0.5 * (next_energy + next_energy.T)
    (next_inv,) = invert(next_energy)
    next_step = mm(next_inv, next_gram)
    near = step + mm(grow, next_step)
    far = mm(step, next_step)
    for c in range(right_ref.shape[0]):
        flat = (-1, size)
        d, q, z, y = [basis_ref[k, c].reshape(flat) for k in range(4)]
        block = right_ref.shape[1:]
        solution_ref[c] = (mm(d, near) - mm(z, far)).reshape(block)
        residual_ref[c] = (right_ref[c].reshape(flat) - mm(q, near) + mm(y, far)).reshape(block)


def finish(grams, right_side, basis):
    vmem = pl.BlockSpec(memory_space=pltpu.VMEM)
    return tuple(
        pl.pallas_call(
            finish_kernel,
            out_shape=[jax.ShapeDtypeStruct(right_side.shape, jnp.float32)] * 2,
            in_specs=[vmem] * 3,
            out_specs=[vmem] * 2,
            name="finish",
        )(grams, right_side, basis)
    )


EDGE = 8
CHANNELS = 8
LOWER, UPPER, BOTH = 0, 1, 2


def krylov_kernel(
    z_lo_count, z_hi_count, right_ref, coef_ref, total_ref, out_ref,
    vec, coef, grams, rs_buf, z_buf,
    halo_send, halo_recv, send, recv, z_send, z_recv, a_send, a_recv,
):
    columns = right_ref.shape[3]
    inner = pl.ds(EDGE, columns)
    group, dev = lax.axis_index("group"), lax.axis_index("dev")
    group_count, dev_count = GROUP_Y * z_lo_count, DEV_XC * z_hi_count
    z_lo, y = group // GROUP_Y, group % GROUP_Y
    z_hi, xc = dev // DEV_XC, dev % DEV_XC
    me = y * DEV_XC + xc
    my_z = z_hi * z_lo_count + z_lo
    z_count = z_lo_count * z_hi_count
    has_prev_dev, has_next_dev = dev > 0, dev < dev_count - 1
    has_prev_group, has_next_group = group > 0, group < group_count - 1
    prev_dev, next_dev = (group, dev - 1), (group, dev + 1)
    prev_group, next_group = (group - 1, dev), (group + 1, dev)

    def plane_peer(step):
        peer = (me + step) % PLANE_PEERS
        return peer, (z_lo * GROUP_Y + peer // DEV_XC, z_hi * DEV_XC + peer % DEV_XC)

    def z_peer(step):
        peer = (my_z + step) % z_count
        return peer, (peer % z_lo_count * GROUP_Y + y, peer // z_lo_count * DEV_XC + xc)

    def clear(line, carry):
        plane, row = line // 4, line % 4
        for v in range(vec.shape[0]):
            vec[v, plane, row] = jnp.zeros(vec.shape[3:], jnp.float32)
        coef[plane, row] = jnp.zeros(coef.shape[2:], jnp.float32)
        return carry

    lax.fori_loop(0, 16, clear, 0)

    def load(line, carry):
        plane, row = line // 2, line % 2
        for c in range(3):
            vec[0, plane + 1, row + 1, c, inner, :] = right_ref[c, plane, row]
        for c in range(2):
            coef[plane + 1, row + 1, c, inner, :] = coef_ref[c, plane, row]
        return carry

    lax.fori_loop(0, 4, load, 0)

    barrier = pltpu.get_barrier_semaphore()

    def greet(place):
        pl.semaphore_signal(barrier, inc=1, device_id=place, device_id_type=MESH)

    def greet_all(count, peer_of):
        def body(step, carry):
            greet(peer_of(step)[1])
            return carry
        lax.fori_loop(1, count, body, 0)

    greet_all(PLANE_PEERS, plane_peer)
    greet_all(z_count, z_peer)
    neighbours = (
        (group, (dev + dev_count - 1) % dev_count), (group, (dev + 1) % dev_count),
        ((group + group_count - 1) % group_count, dev), ((group + 1) % group_count, dev),
    )
    for place in neighbours:
        greet(place)
    pl.semaphore_wait(barrier, PLANE_PEERS - 1 + z_count - 1 + len(neighbours))

    def channel(number, kind):
        down = pl.ds(2, 1) if kind == UPPER else pl.ds(1, 2)
        up = pl.ds(1, 1) if kind == LOWER else pl.ds(1, 2)
        one, rows = (lambda i: pl.ds(i, 1)), pl.ds(1, 2)
        return [
            ((down, one(2)), (down, one(0)), next_dev, has_next_dev, has_prev_dev),
            ((up, one(1)), (up, one(3)), prev_dev, has_prev_dev, has_next_dev),
            ((one(2), rows), (one(0), rows), next_group, has_next_group, has_prev_group),
            ((one(1), rows), (one(3), rows), prev_group, has_prev_group, has_next_group),
            ((one(0), one(2)), (one(0), one(0)), next_dev, has_next_dev & has_prev_group, has_prev_dev & has_prev_group),
            ((one(0), one(1)), (one(0), one(3)), prev_dev, has_prev_dev & has_prev_group, has_next_dev & has_prev_group),
            ((one(3), one(2)), (one(3), one(0)), next_dev, has_next_dev & has_next_group, has_prev_dev & has_next_group),
            ((one(3), one(1)), (one(3), one(3)), prev_dev, has_prev_dev & has_next_group, has_next_dev & has_next_group),
        ][number]

    def halo(buf, phase, number, kind, method):
        (src_plane, src_row), (dst_plane, dst_row), place, to, come = channel(number, kind)

        @pl.when(come if method == "wait_recv" else to)
        def _():
            copy = pltpu.make_async_remote_copy(
                src_ref=buf.at[src_plane, src_row, :, inner, :],
                dst_ref=buf.at[dst_plane, dst_row, :, inner, :],
                send_sem=halo_send.at[phase, number], recv_sem=halo_recv.at[phase, number],
                device_id=place, device_id_type=MESH,
            )
            getattr(copy, method)()

    planes_of = {LOWER: (2,), UPPER: (3,), BOTH: (2, 3)}
    corners_of = {LOWER: (4, 5), UPPER: (6, 7), BOTH: (4, 5, 6, 7)}

    def send_own(buf, phase, kind):
        for number in planes_of[kind] + (0, 1):
            halo(buf, phase, number, kind, "start")

    def take_rims(buf, phase, kind):
        for number in (0, 1):
            halo(buf, phase, number, kind, "wait_recv")

    def pass_planes(buf, phase, kind):
        for number in planes_of[kind]:
            halo(buf, phase, number, kind, "wait_recv")
        for number in corners_of[kind]:
            halo(buf, phase, number, kind, "start")

    def take_corners(buf, phase, kind):
        for number in corners_of[kind]:
            halo(buf, phase, number, kind, "wait_recv")

    def settle(buf, phase, kind):
        for number in (0, 1) + planes_of[kind] + corners_of[kind]:
            halo(buf, phase, number, kind, "wait_send")

    def accumulate(acc, source, which, upper, diagonal, plane, row):
        slots = ([((0, 0, 0), None)] if diagonal else []) + list(zip(lower_offsets, range(len(lower_offsets))))
        for (a, b, c), slot in slots:
            sign = -1 if upper else 1
            at_plane, at_row = plane + 1 + sign * a, row + 1 + sign * b
            cols = pl.ds(EDGE + sign * c, columns)
            blocks = coef[at_plane, at_row, which, cols, :] if upper else coef[plane + 1, row + 1, which, inner, :]
            for j in range(3):
                value = source[at_plane, at_row, j, cols, :]
                for i in range(3):
                    entry = (j * 3 + i) if upper else (i * 3 + j)
                    lane = entry if slot is None else 9 + entry * len(lower_offsets) + slot
                    acc[i] = acc[i] + blocks[:, lane : lane + 1] * value
        return acc

    def apply(source, target, which, kind, between):
        def body(line, carry):
            row, late = line % 2, line // 2

            @pl.when(line == 2)
            def _():
                between()

            parts = {LOWER: ((False, 1 - late, True),), UPPER: ((True, late, True),), BOTH: ((False, 1 - late, True), (True, late, False))}[kind]
            for upper, plane, diagonal in parts:
                old = [target[plane + 1, row + 1, i, inner, :] for i in range(3)]
                new = accumulate(old, source, which, upper, diagonal, plane, row)
                for i in range(3):
                    target[plane + 1, row + 1, i, inner, :] = new[i]
            return carry

        lax.fori_loop(0, 4, body, 0)

    def rows_of(v):
        both = pl.ds(1, 2)
        block = vec[v, both, both, :, inner, :]
        return block.reshape(-1, block.shape[-1])

    def gram(index, left, right):
        left = rows_of(left)
        right = left if right is None else rows_of(right)
        value = mm(left, right, ((0,), (0,)))
        count = value.shape[0] // grams.shape[1]
        grams[pl.ds(index * count, count)] = value.reshape((count,) + grams.shape[1:])

    coef_phase = 6
    send_own(vec.at[0], 0, LOWER)
    send_own(coef, coef_phase, UPPER)

    def round_body(t, carry):
        v = 3 * t
        source, weighted, direction, product = [vec.at[v + k] for k in range(4)]
        f = 3 * t

        @pl.when(t == 1)
        def _():
            send_own(source, f, LOWER)
            gram(1, 2, 3)

        take_rims(source, f, LOWER)

        def planes_lower():
            pass_planes(source, f, LOWER)

            @pl.when(t == 0)
            def _():
                pass_planes(coef, coef_phase, UPPER)
            take_corners(source, f, LOWER)

        apply(source, weighted, 0, LOWER, planes_lower)

        send_own(weighted, f + 1, UPPER)
        gram(2 * t, v + 1, None)
        take_rims(weighted, f + 1, UPPER)

        @pl.when(t == 0)
        def _():
            take_rims(coef, coef_phase, UPPER)
            take_corners(coef, coef_phase, UPPER)

        def planes_upper():
            pass_planes(weighted, f + 1, UPPER)
            take_corners(weighted, f + 1, UPPER)

        apply(weighted, direction, 0, UPPER, planes_upper)

        send_own(direction, f + 2, BOTH)
        take_rims(direction, f + 2, BOTH)

        def planes_both():
            pass_planes(direction, f + 2, BOTH)
            take_corners(direction, f + 2, BOTH)

        apply(direction, product, 1, BOTH, planes_both)

        settle(source, f, LOWER)
        settle(weighted, f + 1, UPPER)
        settle(direction, f + 2, BOTH)
        return carry

    lax.fori_loop(0, 2, round_body, 0)
    settle(coef, coef_phase, UPPER)
    gram(3, 5, 6)

    def scatter(step):
        peer, place = plane_peer(step)
        return pltpu.make_async_remote_copy(
            src_ref=grams.at[peer], dst_ref=rs_buf.at[me], send_sem=send.at[step],
            recv_sem=recv.at[step], device_id=place, device_id_type=MESH,
        )

    def exchange(step):
        _, place = z_peer(step)
        return pltpu.make_async_remote_copy(
            src_ref=z_buf.at[my_z], dst_ref=z_buf.at[my_z], send_sem=z_send.at[step],
            recv_sem=z_recv.at[step], device_id=place, device_id_type=MESH,
        )

    def gather(step):
        _, place = plane_peer(step)
        return pltpu.make_async_remote_copy(
            src_ref=total_ref.at[me], dst_ref=total_ref.at[me], send_sem=a_send.at[step],
            recv_sem=a_recv.at[step], device_id=place, device_id_type=MESH,
        )

    def run(count, make, method):
        def body(step, carry):
            getattr(make(step), method)()
            return carry
        lax.fori_loop(1, count, body, 0)

    run(PLANE_PEERS, scatter, "start")
    rs_buf[me] = grams[me]

    def emit(line, carry):
        plane, row = line // 2, line % 2
        for slot, v in enumerate((2, 3, 5, 6)):
            for c in range(3):
                out_ref[slot, c, plane, row] = vec[v, plane + 1, row + 1, c, inner, :]
        return carry

    lax.fori_loop(0, 4, emit, 0)
    run(PLANE_PEERS, scatter, "wait_recv")
    z_buf[my_z] = jnp.sum(rs_buf[...], axis=0)
    run(z_count, exchange, "start")
    run(z_count, exchange, "wait_recv")
    total_ref[me] = jnp.sum(z_buf[...], axis=0)
    run(PLANE_PEERS, gather, "start")
    run(PLANE_PEERS, gather, "wait_recv")
    run(PLANE_PEERS, scatter, "wait_send")
    run(z_count, exchange, "wait_send")
    run(PLANE_PEERS, gather, "wait_send")


def krylov(right_side, coefs):
    z_lo_count = lax.axis_size("group") // GROUP_Y
    z_hi_count = lax.axis_size("dev") // DEV_XC
    z_count = z_lo_count * z_hi_count
    columns, size = right_side.shape[3:]
    pieces = (PLANE_PEERS, 4 * size // PLANE_PEERS, size)
    wide = columns + 2 * EDGE
    vmem = pl.BlockSpec(memory_space=pltpu.VMEM)
    dma = pltpu.SemaphoreType.DMA
    total, vectors = pl.pallas_call(
        functools.partial(krylov_kernel, z_lo_count, z_hi_count),
        out_shape=[
            jax.ShapeDtypeStruct(pieces, jnp.float32),
            jax.ShapeDtypeStruct((4,) + right_side.shape, jnp.float32),
        ],
        in_specs=[vmem] * 2,
        out_specs=[vmem] * 2,
        scratch_shapes=[
            pltpu.VMEM((7, 4, 4, 3, wide, size), jnp.float32),
            pltpu.VMEM((4, 4, 2, wide, size), jnp.float32),
            pltpu.VMEM(pieces, jnp.float32),
            pltpu.VMEM(pieces, jnp.float32),
            pltpu.VMEM((z_count,) + pieces[1:], jnp.float32),
            dma((7, CHANNELS)), dma((7, CHANNELS)),
            dma((PLANE_PEERS,)), dma((PLANE_PEERS,)),
            dma((z_count,)), dma((z_count,)),
            dma((PLANE_PEERS,)), dma((PLANE_PEERS,)),
        ],
        compiler_params=pltpu.CompilerParams(collective_id=0, has_side_effects=True),
        name="krylov",
    )(right_side, coefs)
    return total.reshape(4 * size, size), vectors


def per_device(right_side, stiff_diag, stiff_lower, fsai_diag, fsai_lower, fsai_pattern):
    planes, rows, columns = right_side.shape[1:4]
    kept = fsai_pattern.astype(jnp.float32)

    def by_node(diag, lower):
        entries = jnp.concatenate([diag.reshape((9,) + diag.shape[2:]), lower.reshape((-1,) + lower.shape[3:])])
        entries = jnp.pad(entries, ((0, right_side.shape[4] - entries.shape[0]), (0, 0), (0, 0)))
        return jnp.transpose(entries, (1, 2, 0)).reshape(planes, rows, columns, -1)

    coefs = jnp.stack([by_node(fsai_diag, fsai_lower * kept[None, None]), by_node(stiff_diag, stiff_lower)])
    return finish_of(right_side, krylov(right_side, coefs))


def finish_of(right_side, reduced):
    grams, basis = reduced
    return finish(grams, right_side, basis)


def solution(mesh):
    return jax.shard_map(
        per_device,
        mesh=mesh,
        in_specs=(
            P(None, "group", "dev", None, None),
            P(None, None, "group", "dev"),
            P(None, None, None, "group", "dev"),
            P(None, None, "group", "dev"),
            P(None, None, None, "group", "dev"),
            P(None, "group", "dev"),
        ),
        out_specs=(P(None, "group", "dev", None, None), P(None, "group", "dev", None, None)),
        check_vma=False,
    )
```

time: 1080 us -> 207 us (0.19)
  waiting for transfers between devices: 788 us -> 0 us
  Pallas kernels: 0 us -> 201 us
  other arithmetic: 168 us -> 2.58 us
  starting transfers between devices: 65.3 us -> 0 us
  between operations: 19.7 us -> 0.67 us
  local copies, waits for them, and re-layouts: 17.9 us -> 2.72 us
  matrix products: 12.7 us -> 0 us
    psum x3 -> x0, waiting for transfers between devices: 752 us -> none  [the longest x2 503 us: residual_sum(): return lax.psum(local_gram(weighted, weighted), ('group', 'dev'))]
    pallas_call x0 -> x2, Pallas kernels: none -> 201 us  [the longest x1 166 us: krylov(): pl.pallas_call(functools.partial(krylov_kernel, z_lo_count, z_hi_count),...]
    add x114 -> x0, other arithmetic: 92.9 us -> none  [the longest x55 42.9 us: block_mul(): coeffs[target, 0][..., None] * vector[0]]
    another operation x15 -> x1, other arithmetic: 69.1 us -> 0.72 us  [per_device(): jnp.stack([by_node(fsai_diag, fsai_lower * kept[None, None]), by_node(sti...]
    ppermute x24 -> x0, starting transfers between devices: 65 us -> none  [the longest x8 32.3 us: with_halo(): lax.ppermute(lax.slice_in_dim(block, block.shape[dim] - width, None, axis...]
    ppermute x24 -> x0, waiting for transfers between devices: 35.9 us -> none  [the longest x8 21.7 us: from_behind(): lax.ppermute(value, axis, [(source, source + steps) for source in range(f...]
  transfers between devices with their start and end apart: 27 -> 0, of which waited for: 13 -> 0; matrix products, arithmetic and copies ran while one was open for 7% -> 0% of each run, Pallas kernels for 0% -> 0%
where the time goes in v1:
time: 207 us
  Pallas kernels  201 us (97%)
  local copies, waits for them, and re-layouts  2.72 us (1%)
  other arithmetic  2.58 us (1%)
    pallas_call x1, Pallas kernels, krylov(): pl.pallas_call(functools.partial(krylov_kernel, z_lo_count, z_hi_count),...  166 us
    pallas_call x1, Pallas kernels, finish(): pl.pallas_call(finish_kernel, out_shape=[jax.ShapeDtypeStruct(right_side....  35 us

profile of v1, /device:TPU:1, one launch (start us, length us, event | category | flops | bytes accessed | tf_op | source)
XLA Modules:
  0.0 207.1 jit_solution(12712308930945133403)
XLA Ops:
  0.6 0.7 convert_element_type.6
  1.3 0.9 broadcast_multiply_fusion
  2.3 0.1 copy.9
  2.4 0.8 copy.10
  3.2 1.0 copy.11
  4.2 0.1 select_maximum_fusion
  4.3 0.8 copy.8
  5.1 0.1 select_maximum_fusion.1
  5.2 0.7 pad_maximum_fusion.coef_ref
  6.0 166.1 %krylov.1 = (f32[32,16,128]{2,1,0:T(8,128)}, f32[4,3,2,2,64,128]{5,4,3,2,1,0:T(8,128)}) custom-call(f32[3,2,2,64,128]{4,3,2,1,0:T(8,128)} %right_ref.3, f32[2,2,2,64,128]{4,3,2,1,0:T(8,128)} %pad_maximum_fusion.coef_ref), custom_call_target="tpu_custom_call" | custom-call | tf_op jit(solution)/shard_map/krylov/pallas_call | solution.py:369
  172.1 35.0 %finish.1 = (f32[3,2,2,64,128]{4,3,2,1,0:T(8,128)}, f32[3,2,2,64,128]{4,3,2,1,0:T(8,128)}) custom-call(f32[512,128]{1,0:T(8,128)} %bitcast.14, f32[3,2,2,64,128]{4,3,2,1,0:T(8,128)} %right_ref.3, f32[4,3,2,2,64,128]{5,4,3,2,1,0:T(8,128)} %get-tuple-element.5.basis_ref), custom_call_target="tpu_custom_call" | custom-call | tf_op jit(solution)/shard_map/finish/pallas_call | solution.py:71

commit v2 on v1

v2 whole, which is shorter than its diff:
```python
import functools

import jax
import jax.numpy as jnp
from jax import lax
from jax.experimental import pallas as pl
from jax.experimental.pallas import tpu as pltpu
from jax.sharding import PartitionSpec as P

MESH = pl.DeviceIdType.MESH
highest = lax.Precision.HIGHEST
GROUP_Y = 4
DEV_XC = 8
PLANE_PEERS = GROUP_Y * DEV_XC
lower_offsets = [(0, 0, -1), (0, -1, -1), (0, -1, 0), (0, -1, 1)] + [
    (-1, row_step, column_step) for row_step in (-1, 0, 1) for column_step in (-1, 0, 1)
]


def mm(left, right, dims=((1,), (0,))):
    return lax.dot_general(left, right, (dims, ((), ())), precision=highest, preferred_element_type=jnp.float32)


TRANS = ((0,), (0,))


def sweep(matrix, row_id, column_id):
    def body(k, m):
        on_row, on_column = row_id == k, column_id == k
        row = jnp.sum(jnp.where(on_row, m, 0.0), axis=0, keepdims=True)
        column = jnp.sum(jnp.where(on_column, m, 0.0), axis=1, keepdims=True)
        pivot = jnp.sum(jnp.where(on_row & on_column, m, 0.0), axis=(0, 1), keepdims=True)
        row = jnp.where(on_column[:1], 1.0, row) / pivot
        swept = jnp.where(on_column, 0.0, m) - column * row
        return jnp.where(on_row, jnp.broadcast_to(row, m.shape), swept)

    return lax.fori_loop(0, matrix.shape[0], body, matrix)


def invert(scratch, *matrices):
    size = matrices[0].shape[0]
    row_id = lax.broadcasted_iota(jnp.int32, (size, size), 0)
    column_id = lax.broadcasted_iota(jnp.int32, (size, size), 1)
    eye = row_id == column_id
    identity = eye.astype(jnp.float32)
    scales, scaled = [], []
    for i, m in enumerate(matrices):
        diag = jnp.where(eye, m, 0.0)
        down = lax.rsqrt(jnp.sum(diag, axis=1, keepdims=True))
        across = lax.rsqrt(jnp.sum(diag, axis=0, keepdims=True))
        scales.append((down, across))
        unit = m * down * across
        scaled.append(unit)
        bound = jnp.max(jnp.sum(jnp.abs(unit), axis=0, keepdims=True), axis=1, keepdims=True)
        gain = 2.0 / (1.0 + bound)
        scratch[i] = gain * (2.0 * identity - gain * unit)

    def more(state):
        count, error = state
        return (error > 1e-8) & (count < 16)

    def newton(state):
        error = 0.0
        for i, unit in enumerate(scaled):
            guess = scratch[i]
            miss = identity - mm(unit, guess)
            scratch[i] = guess + mm(guess, miss)
            error = jnp.maximum(error, jnp.sum(miss * miss))
        return state[0] + 1, error

    _, error = lax.while_loop(more, newton, (0, jnp.float32(1.0)))

    @pl.when(jnp.logical_not(error <= 1e-8))
    def _():
        for i, unit in enumerate(scaled):
            scratch[i] = sweep(unit, row_id, column_id)

    return [scratch[i] * down * across for i, (down, across) in enumerate(scales)]


def finish_kernel(grams_ref, right_ref, basis_ref, solution_ref, residual_ref, scratch):
    size = grams_ref.shape[1]
    resid, energy, coupling, outer = [grams_ref[i * size : (i + 1) * size, :] for i in range(4)]
    identity = (
        lax.broadcasted_iota(jnp.int32, (size, size), 0) == lax.broadcasted_iota(jnp.int32, (size, size), 1)
    ).astype(jnp.float32)
    energy = 0.5 * (energy + energy.T)
    energy_inv, resid_inv = invert(scratch, energy, resid)
    step = mm(energy_inv, resid)
    shift = mm(energy, step)
    coupled = mm(coupling, step)
    next_gram = resid - shift - shift.T + mm(step, coupled, TRANS)
    grow = identity + mm(resid_inv, next_gram)
    cross = mm(grow, coupled, TRANS)
    next_energy = mm(grow, mm(energy, grow), TRANS) - cross - cross.T + mm(step, mm(outer, step), TRANS)
    next_energy = 0.5 * (next_energy + next_energy.T)
    (next_inv,) = invert(scratch, next_energy)
    next_step = mm(next_inv, next_gram)
    near = step + mm(grow, next_step)
    far = mm(step, next_step)
    weights = jnp.concatenate([near.T, -far.T], axis=1)
    planes, comps = basis_ref.shape[1:3]
    for p in range(planes):
        for c in range(comps):
            block = right_ref.shape[2:]
            ahead = mm(weights, jnp.concatenate([basis_ref[0, p, c], basis_ref[2, p, c]]))
            drop = mm(weights, jnp.concatenate([basis_ref[1, p, c], basis_ref[3, p, c]]))
            solution_ref[c, p] = ahead.T.reshape(block)
            residual_ref[c, p] = right_ref[c, p] - drop.T.reshape(block)


def finish(grams, right_side, basis):
    vmem = pl.BlockSpec(memory_space=pltpu.VMEM)
    return tuple(
        pl.pallas_call(
            finish_kernel,
            out_shape=[jax.ShapeDtypeStruct(right_side.shape, jnp.float32)] * 2,
            in_specs=[vmem] * 3,
            out_specs=[vmem] * 2,
            scratch_shapes=[pltpu.VMEM((2, grams.shape[1], grams.shape[1]), jnp.float32)],
            name="finish",
        )(grams, right_side, basis)
    )


CHANNELS = 8
LOWER, UPPER, BOTH = 0, 1, 2
SLOTS = len(lower_offsets)
PHASES = 6


def krylov_kernel(
    z_lo_count, z_hi_count, right_ref, coef_ref, total_ref, out_ref,
    vec, edge, rim_out, rim_in, low, high, low_out, low_in, grams, rs_buf, z_buf,
    halo_send, halo_recv, send, recv, z_send, z_recv, a_send, a_recv,
):
    size, lanes = vec.shape[3:]
    half, top, bottom = lanes // 2, pl.ds(0, size // 2), pl.ds(size // 2, size // 2)
    group, dev = lax.axis_index("group"), lax.axis_index("dev")
    group_count, dev_count = GROUP_Y * z_lo_count, DEV_XC * z_hi_count
    z_lo, y = group // GROUP_Y, group % GROUP_Y
    z_hi, xc = dev // DEV_XC, dev % DEV_XC
    me = y * DEV_XC + xc
    my_z = z_hi * z_lo_count + z_lo
    z_count = z_lo_count * z_hi_count
    has_prev_dev, has_next_dev = dev > 0, dev < dev_count - 1
    has_prev_group, has_next_group = group > 0, group < group_count - 1
    prev_dev, next_dev = (group, dev - 1), (group, dev + 1)
    prev_group, next_group = (group - 1, dev), (group + 1, dev)

    def plane_peer(step):
        peer = (me + step) % PLANE_PEERS
        return peer, (z_lo * GROUP_Y + peer // DEV_XC, z_hi * DEV_XC + peer % DEV_XC)

    def z_peer(step):
        peer = (my_z + step) % z_count
        return peer, (peer % z_lo_count * GROUP_Y + y, peer // z_lo_count * DEV_XC + xc)

    def clear(ref):
        ref[...] = jnp.zeros(ref.shape, ref.dtype)

    def clear_phases(*refs_of):
        def body(f, carry):
            for ref_of in refs_of:
                clear(ref_of(f))
            return carry
        lax.fori_loop(0, PHASES, body, 0)

    @pl.when(jnp.logical_not(has_prev_dev))
    def _():
        clear_phases(lambda f: rim_in.at[f, 0])
        clear(low_in.at[0])

    @pl.when(jnp.logical_not(has_next_dev))
    def _():
        clear_phases(lambda f: rim_in.at[f, 1])
        clear(low_in.at[1])

    @pl.when(jnp.logical_not(has_prev_group))
    def _():
        clear_phases(lambda f: rim_in.at[f, 0, 0], lambda f: rim_in.at[f, 1, 0], lambda f: vec.at[f, 0])

    @pl.when(jnp.logical_not(has_next_group))
    def _():
        clear_phases(lambda f: rim_in.at[f, 0, 3], lambda f: rim_in.at[f, 1, 3], lambda f: vec.at[f, 3])
        for k in range(2):
            clear(low_in.at[k, 2])
            clear(low.at[k, 2])

    barrier = pltpu.get_barrier_semaphore()

    def greet(place):
        pl.semaphore_signal(barrier, inc=1, device_id=place, device_id_type=MESH)

    def greet_all(count, peer_of):
        def body(step, carry):
            greet(peer_of(step)[1])
            return carry
        lax.fori_loop(1, count, body, 0)

    neighbours = (
        (group, (dev + dev_count - 1) % dev_count), (group, (dev + 1) % dev_count),
        ((group + group_count - 1) % group_count, dev), ((group + 1) % group_count, dev),
    )
    greet_all(PLANE_PEERS, plane_peer)
    greet_all(z_count, z_peer)
    for place in neighbours:
        greet(place)

    def left_of(shape):
        return lax.broadcasted_iota(jnp.int32, shape, len(shape) - 1) < half

    def swap(tile):
        return pltpu.roll(tile, half, axis=tile.ndim - 1)

    def turn(tile, step):
        return tile if step == 0 else pltpu.roll(tile, -step % lanes, axis=tile.ndim - 1)

    for p in range(2):
        for c in range(3):
            vec[0, p + 1, c] = right_ref[c, p].reshape(lanes, size).T

    left_low = left_of(low.shape[3:])
    left_half = left_of((size // 2, lanes))

    def pack_low(plane):
        low_out[0, plane] = jnp.where(left_low[None], swap(low[0, plane]), low[1, plane])
        low_out[1, plane] = jnp.where(left_low[None], low[0, plane], swap(low[1, plane]))

    for p in range(2):
        for k in range(2):
            low[k, p] = coef_ref[k, p, 1:]
        pack_low(p)
    pl.semaphore_wait(barrier, PLANE_PEERS - 1 + z_count - 1 + len(neighbours))

    def route(number):
        return [
            (next_dev, has_next_dev, has_prev_dev),
            (prev_dev, has_prev_dev, has_next_dev),
            (next_group, has_next_group, has_prev_group),
            (prev_group, has_prev_group, has_next_group),
            (next_dev, has_next_dev & has_prev_group, has_prev_dev & has_prev_group),
            (prev_dev, has_prev_dev & has_prev_group, has_next_dev & has_prev_group),
            (next_dev, has_next_dev & has_next_group, has_prev_dev & has_next_group),
            (prev_dev, has_prev_dev & has_next_group, has_next_dev & has_next_group),
        ][number]

    def move(source, target, phase, number, method):
        place, to, come = route(number)

        @pl.when(come if method == "wait_recv" else to)
        def _():
            copy = pltpu.make_async_remote_copy(
                src_ref=source, dst_ref=target,
                send_sem=halo_send.at[phase, number], recv_sem=halo_recv.at[phase, number],
                device_id=place, device_id_type=MESH,
            )
            getattr(copy, method)()

    def halo(f, number, kind, method):
        if number in (2, 3):
            source, target = (2, 0) if number == 2 else (1, 3)
            move(vec.at[f, source], vec.at[f, target], f, number, method)
            return
        side = number % 2
        if number > 3:
            planes = pl.ds(0 if number < 6 else 3, 1)
        elif side == 0:
            planes = pl.ds(2, 1) if kind == UPPER else pl.ds(1, 2)
        else:
            planes = pl.ds(1, 1) if kind == LOWER else pl.ds(1, 2)
        move(rim_out.at[f, side, planes], rim_in.at[f, side, planes], f, number, method)

    def low_halo(number, method):
        if number == 3:
            move(low.at[:, 0], low.at[:, 2], PHASES, number, method)
            return
        side = number % 2
        planes = pl.ds(2, 1) if number > 3 else (pl.ds(1, 1) if side == 0 else pl.ds(0, 2))
        move(low_out.at[side, planes], low_in.at[side, planes], PHASES, number, method)

    planes_of = {LOWER: (2,), UPPER: (3,), BOTH: (2, 3)}
    corners_of = {LOWER: (4, 5), UPPER: (6, 7), BOTH: (4, 5, 6, 7)}

    def pack(f, plane, sides=(0, 1)):
        for c in range(3):
            upper_rows, lower_rows = vec[f, plane, c, top, :], vec[f, plane, c, bottom, :]
            if 0 in sides:
                rim_out[f, 0, plane, c] = jnp.where(left_half, swap(upper_rows), lower_rows)
            if 1 in sides:
                rim_out[f, 1, plane, c] = jnp.where(left_half, upper_rows, swap(lower_rows))

    def unpack(f, plane):
        for c in range(3):
            before, after = rim_in[f, 0, plane, c], rim_in[f, 1, plane, c]
            edge[plane, c, top, :] = jnp.where(left_half, before, swap(after))
            edge[plane, c, bottom, :] = jnp.where(left_half, swap(before), after)

    def send_own(f, kind):
        for number in planes_of[kind]:
            halo(f, number, kind, "start")
        for plane in (1, 2):
            pack(f, plane)
        for number in (0, 1):
            halo(f, number, kind, "start")

    def take_rims(f, kind):
        for number in (0, 1):
            halo(f, number, kind, "wait_recv")
        for plane in (1, 2):
            unpack(f, plane)

    outer_of = {LOWER: (0,), UPPER: (3,), BOTH: (0, 3)}

    def pass_planes(f, kind):
        for number, plane in zip(planes_of[kind], outer_of[kind]):
            halo(f, number, kind, "wait_recv")
            pack(f, plane)
            for corner in (4, 5) if plane == 0 else (6, 7):
                halo(f, corner, kind, "start")

    def take_corners(f, kind):
        for number in corners_of[kind]:
            halo(f, number, kind, "wait_recv")
        for plane in outer_of[kind]:
            unpack(f, plane)

    def settle(f, kind):
        for number in (0, 1) + planes_of[kind] + corners_of[kind]:
            halo(f, number, kind, "wait_send")

    def raise_coefs(k):
        def body(p, carry):
            for slot, (a, b, c) in enumerate(lower_offsets):
                at = p - a
                base = low[k, at, slot]
                if b == -1:
                    rim = low_in[1, at, slot]
                    base = jnp.where(left_low, swap(base), swap(rim) if k == 0 else rim)
                elif b == 1:
                    rim = low_in[0, at, slot]
                    base = jnp.where(left_low, rim if k == 0 else swap(rim), swap(base))
                high[k, p, slot] = turn(base, -c)
            return carry
        lax.fori_loop(0, 2, body, 0)

    groups = {}
    for slot, (a, b, c) in enumerate(lower_offsets):
        groups.setdefault((a, b), []).append((slot, c))

    rows_count = 32
    left = left_of((rows_count, lanes))

    def accumulate(acc, v, k, upper, diagonal, plane, rows):
        sign = -1 if upper else 1
        swapped = {}
        for (a, b), slots in groups.items():
            at = plane + 1 + sign * a
            for j in range(3):
                tile = vec[v, at, j, rows, :]
                if b != 0:
                    if (a, j) not in swapped:
                        swapped[a, j] = swap(tile)
                    outside = edge[at, j, rows, :]
                    tile = (
                        jnp.where(left, outside, swapped[a, j]) if sign * b < 0
                        else jnp.where(left, swapped[a, j], outside)
                    )
                if diagonal and (a, b) == (0, 0):
                    for i in range(3):
                        entry = j * 3 + i if upper else i * 3 + j
                        acc[i] = acc[i] + coef_ref[k, plane, 0, pl.ds(entry, 1), :] * tile
                for slot, c in slots:
                    value = turn(tile, sign * c)
                    for i in range(3):
                        if upper:
                            block = high[k, plane, slot, pl.ds(j * 3 + i, 1), :]
                        else:
                            block = low[k, plane, slot, pl.ds(i * 3 + j, 1), :]
                        acc[i] = acc[i] + block * value
        return acc

    def apply(v, target, k, kind, between):
        chunks = size // rows_count

        def body(step, carry):
            late = step // chunks
            rows = pl.ds(pl.multiple_of(step % chunks * rows_count, rows_count), rows_count)

            @pl.when(step == chunks)
            def _():
                between()

            parts = {LOWER: ((False, 1 - late, True),), UPPER: ((True, late, True),), BOTH: ((False, 1 - late, True), (True, late, False))}[kind]
            for upper, plane, diagonal in parts:
                acc = [jnp.zeros((rows_count, lanes), jnp.float32)] * 3
                acc = accumulate(acc, v, k, upper, diagonal, plane, rows)
                for i in range(3):
                    if kind == BOTH:
                        acc[i] = jnp.where(late > 0, vec[target, plane + 1, i, rows, :], 0.0) + acc[i]
                    vec[target, plane + 1, i, rows, :] = acc[i]
            return carry

        lax.fori_loop(0, 2 * chunks, body, 0)

    def across(v):
        return jnp.concatenate([vec[v, p, c] for p in (1, 2) for c in range(3)], axis=1)

    def gram(index, v, w):
        one = across(v)
        value = mm(one, one if w is None else across(w), ((1,), (1,)))
        count = value.shape[0] // grams.shape[1]
        grams[pl.ds(index * count, count)] = value.reshape((count,) + grams.shape[1:])

    send_own(0, LOWER)
    for number in (3, 0, 1):
        low_halo(number, "start")

    def round_body(t, carry):
        f = 3 * t

        @pl.when(t == 1)
        def _():
            send_own(f, LOWER)
            gram(1, 2, 3)

        take_rims(f, LOWER)

        def planes_lower():
            pass_planes(f, LOWER)

            @pl.when(t == 0)
            def _():
                low_halo(3, "wait_recv")
                pack_low(2)
                for number in (6, 7):
                    low_halo(number, "start")
            take_corners(f, LOWER)

        apply(f, f + 1, 0, LOWER, planes_lower)

        send_own(f + 1, UPPER)
        gram(2 * t, f + 1, None)

        @pl.when(t == 0)
        def _():
            for number in (0, 1, 6, 7):
                low_halo(number, "wait_recv")
            raise_coefs(0)
        take_rims(f + 1, UPPER)

        def planes_upper():
            pass_planes(f + 1, UPPER)
            take_corners(f + 1, UPPER)

        apply(f + 1, f + 2, 0, UPPER, planes_upper)

        send_own(f + 2, BOTH)

        @pl.when(t == 0)
        def _():
            raise_coefs(1)
        take_rims(f + 2, BOTH)

        def planes_both():
            pass_planes(f + 2, BOTH)
            take_corners(f + 2, BOTH)

        apply(f + 2, f + 3, 1, BOTH, planes_both)

        settle(f, LOWER)
        settle(f + 1, UPPER)
        settle(f + 2, BOTH)
        return carry

    lax.fori_loop(0, 2, round_body, 0)
    for number in (3, 0, 1, 6, 7):
        low_halo(number, "wait_send")
    gram(3, 5, 6)

    def scatter(step):
        peer, place = plane_peer(step)
        return pltpu.make_async_remote_copy(
            src_ref=grams.at[peer], dst_ref=rs_buf.at[me], send_sem=send.at[step],
            recv_sem=recv.at[step], device_id=place, device_id_type=MESH,
        )

    def exchange(step):
        _, place = z_peer(step)
        return pltpu.make_async_remote_copy(
            src_ref=z_buf.at[my_z], dst_ref=z_buf.at[my_z], send_sem=z_send.at[step],
            recv_sem=z_recv.at[step], device_id=place, device_id_type=MESH,
        )

    def gather(step):
        _, place = plane_peer(step)
        return pltpu.make_async_remote_copy(
            src_ref=total_ref.at[me], dst_ref=total_ref.at[me], send_sem=a_send.at[step],
            recv_sem=a_recv.at[step], device_id=place, device_id_type=MESH,
        )

    def run(count, make, method):
        def body(step, carry):
            getattr(make(step), method)()
            return carry
        lax.fori_loop(1, count, body, 0)

    run(PLANE_PEERS, scatter, "start")
    rs_buf[me] = grams[me]
    for slot, v in enumerate((2, 3, 5, 6)):
        for p in range(2):
            out_ref[slot, p] = vec[v, p + 1]
    run(PLANE_PEERS, scatter, "wait_recv")
    z_buf[my_z] = jnp.sum(rs_buf[...], axis=0)
    run(z_count, exchange, "start")
    run(z_count, exchange, "wait_recv")
    total_ref[me] = jnp.sum(z_buf[...], axis=0)
    run(PLANE_PEERS, gather, "start")
    run(PLANE_PEERS, gather, "wait_recv")
    run(PLANE_PEERS, scatter, "wait_send")
    run(z_count, exchange, "wait_send")
    run(PLANE_PEERS, gather, "wait_send")


def krylov(right_side, coefs):
    z_lo_count = lax.axis_size("group") // GROUP_Y
    z_hi_count = lax.axis_size("dev") // DEV_XC
    z_count = z_lo_count * z_hi_count
    comps, planes, rows, columns, size = right_side.shape
    lanes = rows * columns
    pieces = (PLANE_PEERS, 4 * size // PLANE_PEERS, size)
    vmem = pl.BlockSpec(memory_space=pltpu.VMEM)
    dma = pltpu.SemaphoreType.DMA

    def array(*shape):
        return pltpu.VMEM(shape, jnp.float32)

    total, vectors = pl.pallas_call(
        functools.partial(krylov_kernel, z_lo_count, z_hi_count),
        out_shape=[
            jax.ShapeDtypeStruct(pieces, jnp.float32),
            jax.ShapeDtypeStruct((4, planes, comps, size, lanes), jnp.float32),
        ],
        in_specs=[vmem] * 2,
        out_specs=[vmem] * 2,
        scratch_shapes=[
            array(7, 4, comps, size, lanes),
            array(4, comps, size, lanes),
            array(PHASES, 2, 4, comps, size // 2, lanes),
            array(PHASES, 2, 4, comps, size // 2, lanes),
            array(2, 3, SLOTS, 9, lanes),
            array(2, 2, SLOTS, 9, lanes),
            array(2, 3, SLOTS, 9, lanes),
            array(2, 3, SLOTS, 9, lanes),
            array(*pieces),
            array(*pieces),
            array(z_count, *pieces[1:]),
            dma((PHASES + 1, CHANNELS)), dma((PHASES + 1, CHANNELS)),
            dma((PLANE_PEERS,)), dma((PLANE_PEERS,)),
            dma((z_count,)), dma((z_count,)),
            dma((PLANE_PEERS,)), dma((PLANE_PEERS,)),
        ],
        compiler_params=pltpu.CompilerParams(collective_id=0, has_side_effects=True),
        name="krylov",
    )(right_side, coefs)
    return total.reshape(4 * size, size), vectors


def per_device(right_side, stiff_diag, stiff_lower, fsai_diag, fsai_lower, fsai_pattern):
    columns = right_side.shape[3]
    lanes = stiff_diag.shape[3]
    kept = fsai_pattern.astype(jnp.float32)
    steps = jnp.array([c for _, _, c in lower_offsets])[:, None, None]
    column = jnp.arange(lanes)[None, None, :] % columns + steps
    inside = ((column >= 0) & (column < columns)).astype(jnp.float32)

    def by_plane(diag, lower):
        lower = (lower * inside).reshape((9,) + lower.shape[2:])
        entries = jnp.concatenate([diag.reshape((9, 1) + diag.shape[2:]), lower], axis=1)
        return jnp.transpose(entries, (2, 1, 0, 3))

    coefs = jnp.stack([by_plane(fsai_diag, fsai_lower * kept[None, None]), by_plane(stiff_diag, stiff_lower)])
    grams, basis = krylov(right_side, coefs)
    return finish(grams, right_side, basis)


def solution(mesh):
    return jax.shard_map(
        per_device,
        mesh=mesh,
        in_specs=(
            P(None, "group", "dev", None, None),
            P(None, None, "group", "dev"),
            P(None, None, None, "group", "dev"),
            P(None, None, "group", "dev"),
            P(None, None, None, "group", "dev"),
            P(None, "group", "dev"),
        ),
        out_specs=(P(None, "group", "dev", None, None), P(None, "group", "dev", None, None)),
        check_vma=False,
    )
```

time: 207 us -> 161 us (0.78)
  Pallas kernels: 201 us -> 155 us
    pallas_call x1, Pallas kernels: 166 us -> 140 us  [krylov(): pl.pallas_call(functools.partial(krylov_kernel, z_lo_count, z_hi_count),...]
    pallas_call x1, Pallas kernels: 35 us -> 15.7 us  [finish(): pl.pallas_call(finish_kernel, out_shape=[jax.ShapeDtypeStruct(right_side....]
where the time goes in v2:
time: 161 us
  Pallas kernels  155 us (96%)
  other arithmetic  3.36 us (2%)
    pallas_call x1, Pallas kernels, krylov(): pl.pallas_call(functools.partial(krylov_kernel, z_lo_count, z_hi_count),...  140 us
    pallas_call x1, Pallas kernels, finish(): pl.pallas_call(finish_kernel, out_shape=[jax.ShapeDtypeStruct(right_side....  15.7 us

profile of v2, /device:TPU:1, one launch (start us, length us, event | category | flops | bytes accessed | tf_op | source)
XLA Modules:
  0.0 160.8 jit_solution(143269502399883749)
XLA Ops:
  0.6 0.7 fusion.1
  1.4 0.7 convert_element_type.12
  2.1 0.7 copy.15
  2.8 0.7 copy.13
  3.5 1.0 multiply_multiply_fusion
  4.6 0.8 pad_maximum_fusion.coef_ref
  5.5 139.6 %krylov.1 = (f32[32,16,128]{2,1,0:T(8,128)}, f32[4,2,3,128,128]{4,3,2,1,0:T(8,128)}) custom-call(f32[3,2,2,64,128]{4,3,2,1,0:T(8,128)} %right_ref.3, f32[2,2,14,9,128]{4,3,2,1,0:T(8,128)} %pad_maximum_fusion.coef_ref), custom_call_target="tpu_custom_call" | custom-call | tf_op jit(solution)/shard_map/krylov/pallas_call | solution.py:538
  145.1 15.7 %finish.1 = (f32[3,2,2,64,128]{4,3,2,1,0:T(8,128)}, f32[3,2,2,64,128]{4,3,2,1,0:T(8,128)}) custom-call(f32[512,128]{1,0:T(8,128)} %bitcast.15, f32[3,2,2,64,128]{4,3,2,1,0:T(8,128)} %right_ref.3, f32[4,2,3,128,128]{4,3,2,1,0:T(8,128)} %get-tuple-element.5.basis_ref), custom_call_target="tpu_custom_call" | custom-call | tf_op jit(solution)/shard_map/finish/pallas_call | solution.py:115
  (4 shorter events, 0.1 us)

commit v3 on v2

--- a/solution.py
+++ b/solution.py
@@ -123,14 +123,14 @@
     )
 
 
-CHANNELS = 8
+CHANNELS = 12
 LOWER, UPPER, BOTH = 0, 1, 2
 SLOTS = len(lower_offsets)
 PHASES = 6
 
 
 def krylov_kernel(
-    z_lo_count, z_hi_count, right_ref, coef_ref, total_ref, out_ref,
+    z_lo_count, z_hi_count, right_ref, stiff_diag_ref, stiff_ref, fsai_diag_ref, fsai_ref, kept_ref, total_ref, out_ref,
     vec, edge, rim_out, rim_in, low, high, low_out, low_in, grams, rs_buf, z_buf,
     halo_send, halo_recv, send, recv, z_send, z_recv, a_send, a_recv,
 ):
@@ -227,23 +227,33 @@
         low_out[0, plane] = jnp.where(left_low[None], swap(low[0, plane]), low[1, plane])
         low_out[1, plane] = jnp.where(left_low[None], low[0, plane], swap(low[1, plane]))
 
+    column = lax.broadcasted_iota(jnp.int32, (1, lanes), 1) % half
+    inside = {-1: column > 0, 0: column >= 0, 1: column < half - 1}
     for p in range(2):
-        for k in range(2):
-            low[k, p] = coef_ref[k, p, 1:]
+        for slot, (_, _, c) in enumerate(lower_offsets):
+            kept = jnp.where(inside[c], kept_ref[slot, pl.ds(p, 1), :].astype(jnp.float32), 0.0)
+            for i in range(3):
+                for j in range(3):
+                    entry = pl.ds(i * 3 + j, 1)
+                    low[0, p, slot, entry, :] = fsai_ref[i, j, slot, pl.ds(p, 1), :] * kept
+                    low[1, p, slot, entry, :] = jnp.where(inside[c], stiff_ref[i, j, slot, pl.ds(p, 1), :], 0.0)
         pack_low(p)
     pl.semaphore_wait(barrier, PLANE_PEERS - 1 + z_count - 1 + len(neighbours))
 
     def route(number):
-        return [
-            (next_dev, has_next_dev, has_prev_dev),
-            (prev_dev, has_prev_dev, has_next_dev),
-            (next_group, has_next_group, has_prev_group),
-            (prev_group, has_prev_group, has_next_group),
-            (next_dev, has_next_dev & has_prev_group, has_prev_dev & has_prev_group),
-            (prev_dev, has_prev_dev & has_prev_group, has_next_dev & has_prev_group),
-            (next_dev, has_next_dev & has_next_group, has_prev_dev & has_next_group),
-            (prev_dev, has_prev_dev & has_next_group, has_next_dev & has_next_group),
-        ][number]
+        along = {
+            0: (next_dev, has_next_dev, has_prev_dev),
+            1: (prev_dev, has_prev_dev, has_next_dev),
+            2: (next_group, has_next_group, has_prev_group),
+            3: (prev_group, has_prev_group, has_next_group),
+        }
+        if number < 2:
+            return along[number]
+        if number < 8:
+            return along[2 if number < 5 else 3]
+        place, to, come = along[number % 2]
+        given = has_prev_group if number < 10 else has_next_group
+        return place, to & given, come & given
 
     def move(source, target, phase, number, method):
         place, to, come = route(number)
@@ -257,38 +267,33 @@
             )
             getattr(copy, method)()
 
-    def halo(f, number, kind, method):
-        if number in (2, 3):
-            source, target = (2, 0) if number == 2 else (1, 3)
-            move(vec.at[f, source], vec.at[f, target], f, number, method)
-            return
-        side = number % 2
-        if number > 3:
-            planes = pl.ds(0 if number < 6 else 3, 1)
-        elif side == 0:
+    def halo_plane(f, plane, c, method):
+        number, source = (2, 2) if plane == 0 else (5, 1)
+        move(vec.at[f, source, c], vec.at[f, plane, c], f, number + c, method)
+
+    def halo_rim(f, side, kind, method):
+        if side == 0:
             planes = pl.ds(2, 1) if kind == UPPER else pl.ds(1, 2)
         else:
             planes = pl.ds(1, 1) if kind == LOWER else pl.ds(1, 2)
-        move(rim_out.at[f, side, planes], rim_in.at[f, side, planes], f, number, method)
+        move(rim_out.at[f, side, planes], rim_in.at[f, side, planes], f, side, method)
+
+    def halo_corner(f, plane, side, method, comps=pl.ds(0, 3)):
+        number = (8 if plane == 0 else 10) + side
+        move(rim_out.at[f, side, plane, comps], rim_in.at[f, side, plane, comps], f, number, method)
 
     def low_halo(number, method):
-        if number == 3:
+        if number == 5:
             move(low.at[:, 0], low.at[:, 2], PHASES, number, method)
             return
         side = number % 2
-        planes = pl.ds(2, 1) if number > 3 else (pl.ds(1, 1) if side == 0 else pl.ds(0, 2))
+        planes = pl.ds(2, 1) if number > 5 else (pl.ds(1, 1) if side == 0 else pl.ds(0, 2))
         move(low_out.at[side, planes], low_in.at[side, planes], PHASES, number, method)
 
-    planes_of = {LOWER: (2,), UPPER: (3,), BOTH: (2, 3)}
-    corners_of = {LOWER: (4, 5), UPPER: (6, 7), BOTH: (4, 5, 6, 7)}
-
-    def pack(f, plane, sides=(0, 1)):
-        for c in range(3):
-            upper_rows, lower_rows = vec[f, plane, c, top, :], vec[f, plane, c, bottom, :]
-            if 0 in sides:
-                rim_out[f, 0, plane, c] = jnp.where(left_half, swap(upper_rows), lower_rows)
-            if 1 in sides:
-                rim_out[f, 1, plane, c] = jnp.where(left_half, upper_rows, swap(lower_rows))
+    def pack(f, plane, c):
+        upper_rows, lower_rows = vec[f, plane, c, top, :], vec[f, plane, c, bottom, :]
+        rim_out[f, 0, plane, c] = jnp.where(left_half, swap(upper_rows), lower_rows)
+        rim_out[f, 1, plane, c] = jnp.where(left_half, upper_rows, swap(lower_rows))
 
     def unpack(f, plane):
         for c in range(3):
@@ -296,38 +301,46 @@
             edge[plane, c, top, :] = jnp.where(left_half, before, swap(after))
             edge[plane, c, bottom, :] = jnp.where(left_half, swap(before), after)
 
+    outer_of = {LOWER: (0,), UPPER: (3,), BOTH: (0, 3)}
+
     def send_own(f, kind):
-        for number in planes_of[kind]:
-            halo(f, number, kind, "start")
+        for c in range(3):
+            for plane in outer_of[kind]:
+                halo_plane(f, plane, c, "start")
         for plane in (1, 2):
-            pack(f, plane)
-        for number in (0, 1):
-            halo(f, number, kind, "start")
+            for c in range(3):
+                pack(f, plane, c)
+        for side in (0, 1):
+            halo_rim(f, side, kind, "start")
+
+    def pass_planes(f, kind):
+        for c in range(3):
+            for plane in outer_of[kind]:
+                halo_plane(f, plane, c, "wait_recv")
+                pack(f, plane, c)
+                for side in (0, 1):
+                    halo_corner(f, plane, side, "start", pl.ds(c, 1))
 
     def take_rims(f, kind):
-        for number in (0, 1):
-            halo(f, number, kind, "wait_recv")
+        for side in (0, 1):
+            halo_rim(f, side, kind, "wait_recv")
         for plane in (1, 2):
             unpack(f, plane)
 
-    outer_of = {LOWER: (0,), UPPER: (3,), BOTH: (0, 3)}
-
-    def pass_planes(f, kind):
-        for number, plane in zip(planes_of[kind], outer_of[kind]):
-            halo(f, number, kind, "wait_recv")
-            pack(f, plane)
-            for corner in (4, 5) if plane == 0 else (6, 7):
-                halo(f, corner, kind, "start")
-
     def take_corners(f, kind):
-        for number in corners_of[kind]:
-            halo(f, number, kind, "wait_recv")
         for plane in outer_of[kind]:
+            for side in (0, 1):
+                halo_corner(f, plane, side, "wait_recv")
             unpack(f, plane)
 
     def settle(f, kind):
-        for number in (0, 1) + planes_of[kind] + corners_of[kind]:
-            halo(f, number, kind, "wait_send")
+        for side in (0, 1):
+            halo_rim(f, side, kind, "wait_send")
+            for plane in outer_of[kind]:
+                halo_corner(f, plane, side, "wait_send")
+        for plane in outer_of[kind]:
+            for c in range(3):
+                halo_plane(f, plane, c, "wait_send")
 
     def raise_coefs(k):
         def body(p, carry):
@@ -344,64 +357,58 @@
             return carry
         lax.fori_loop(0, 2, body, 0)
 
-    groups = {}
-    for slot, (a, b, c) in enumerate(lower_offsets):
-        groups.setdefault((a, b), []).append((slot, c))
-
     rows_count = 32
     left = left_of((rows_count, lanes))
-
-    def accumulate(acc, v, k, upper, diagonal, plane, rows):
-        sign = -1 if upper else 1
-        swapped = {}
-        for (a, b), slots in groups.items():
-            at = plane + 1 + sign * a
+    diags = (fsai_diag_ref, stiff_diag_ref)
+
+    def uses_of(parts):
+        uses = {}
+        for part, (upper, plane, diagonal) in enumerate(parts):
+            sign = -1 if upper else 1
+            slots = [(None, (0, 0, 0))] if diagonal else []
+            for slot, (a, b, c) in slots + list(enumerate(lower_offsets)):
+                at = uses.setdefault(plane + 1 + sign * a, {}).setdefault(sign * b, {})
+                at.setdefault(sign * c, []).append((part, slot))
+        return uses
+
+    def accumulate(acc, v, k, parts, rows):
+        for at, by_row in sorted(uses_of(parts).items()):
             for j in range(3):
-                tile = vec[v, at, j, rows, :]
-                if b != 0:
-                    if (a, j) not in swapped:
-                        swapped[a, j] = swap(tile)
-                    outside = edge[at, j, rows, :]
-                    tile = (
-                        jnp.where(left, outside, swapped[a, j]) if sign * b < 0
-                        else jnp.where(left, swapped[a, j], outside)
-                    )
-                if diagonal and (a, b) == (0, 0):
-                    for i in range(3):
-                        entry = j * 3 + i if upper else i * 3 + j
-                        acc[i] = acc[i] + coef_ref[k, plane, 0, pl.ds(entry, 1), :] * tile
-                for slot, c in slots:
-                    value = turn(tile, sign * c)
-                    for i in range(3):
-                        if upper:
-                            block = high[k, plane, slot, pl.ds(j * 3 + i, 1), :]
-                        else:
-                            block = low[k, plane, slot, pl.ds(i * 3 + j, 1), :]
-                        acc[i] = acc[i] + block * value
+                own = vec[v, at, j, rows, :]
+                swapped = swap(own) if set(by_row) != {0} else None
+                for b, by_column in sorted(by_row.items()):
+                    tile = own
+                    if b != 0:
+                        outside = edge[at, j, rows, :]
+                        tile = jnp.where(left, outside, swapped) if b < 0 else jnp.where(left, swapped, outside)
+                    for c, users in sorted(by_column.items()):
+                        value = turn(tile, c)
+                        for part, slot in users:
+                            upper, plane, _ = parts[part]
+                            for i in range(3):
+                                row, col = (j, i) if upper else (i, j)
+                                if slot is None:
+                                    block = diags[k][row, col, pl.ds(plane, 1), :]
+                                else:
+                                    table = high if upper else low
+                                    block = table[k, plane, slot, pl.ds(row * 3 + col, 1), :]
+                                acc[part][i] = acc[part][i] + block * value
         return acc
 
-    def apply(v, target, k, kind, between):
-        chunks = size // rows_count
-
+    def apply(v, target, k, parts, add):
         def body(step, carry):
-            late = step // chunks
-            rows = pl.ds(pl.multiple_of(step % chunks * rows_count, rows_count), rows_count)
-
-            @pl.when(step == chunks)
-            def _():
-                between()
-
-            parts = {LOWER: ((False, 1 - late, True),), UPPER: ((True, late, True),), BOTH: ((False, 1 - late, True), (True, late, False))}[kind]
-            for upper, plane, diagonal in parts:
-                acc = [jnp.zeros((rows_count, lanes), jnp.float32)] * 3
-                acc = accumulate(acc, v, k, upper, diagonal, plane, rows)
+            rows = pl.ds(pl.multiple_of(step * rows_count, rows_count), rows_count)
+            if add:
+                acc = [[vec[target, plane + 1, i, rows, :] for i in range(3)] for _, plane, _ in parts]
+            else:
+                acc = [[jnp.zeros((rows_count, lanes), jnp.float32)] * 3 for _ in parts]
+            acc = accumulate(acc, v, k, parts, rows)
+            for (_, plane, _), values in zip(parts, acc):
                 for i in range(3):
-                    if kind == BOTH:
-                        acc[i] = jnp.where(late > 0, vec[target, plane + 1, i, rows, :], 0.0) + acc[i]
-                    vec[target, plane + 1, i, rows, :] = acc[i]
+                    vec[target, plane + 1, i, rows, :] = values[i]
             return carry
 
-        lax.fori_loop(0, 2 * chunks, body, 0)
+        lax.fori_loop(0, size // rows_count, body, 0, unroll=2)
 
     def across(v):
         return jnp.concatenate([vec[v, p, c] for p in (1, 2) for c in range(3)], axis=1)
@@ -413,7 +420,7 @@
         grams[pl.ds(index * count, count)] = value.reshape((count,) + grams.shape[1:])
 
     send_own(0, LOWER)
-    for number in (3, 0, 1):
+    for number in (5, 0, 1):
         low_halo(number, "start")
 
     def round_body(t, carry):
@@ -424,49 +431,46 @@
             send_own(f, LOWER)
             gram(1, 2, 3)
 
+        pass_planes(f, LOWER)
+
+        @pl.when(t == 0)
+        def _():
+            low_halo(5, "wait_recv")
+            pack_low(2)
+            for number in (10, 11):
+                low_halo(number, "start")
+
         take_rims(f, LOWER)
-
-        def planes_lower():
-            pass_planes(f, LOWER)
-
-            @pl.when(t == 0)
-            def _():
-                low_halo(3, "wait_recv")
-                pack_low(2)
-                for number in (6, 7):
-                    low_halo(number, "start")
-            take_corners(f, LOWER)
-
-        apply(f, f + 1, 0, LOWER, planes_lower)
+        apply(f, f + 1, 0, ((False, 1, True),), False)
+        take_corners(f, LOWER)
+        apply(f, f + 1, 0, ((False, 0, True),), False)
 
         send_own(f + 1, UPPER)
         gram(2 * t, f + 1, None)
 
         @pl.when(t == 0)
         def _():
-            for number in (0, 1, 6, 7):
+            for number in (0, 1, 10, 11):
                 low_halo(number, "wait_recv")
             raise_coefs(0)
+
+        pass_planes(f + 1, UPPER)
         take_rims(f + 1, UPPER)
-
-        def planes_upper():
-            pass_planes(f + 1, UPPER)
-            take_corners(f + 1, UPPER)
-
-        apply(f + 1, f + 2, 0, UPPER, planes_upper)
+        apply(f + 1, f + 2, 0, ((True, 0, True),), False)
+        take_corners(f + 1, UPPER)
+        apply(f + 1, f + 2, 0, ((True, 1, True),), False)
 
         send_own(f + 2, BOTH)
 
         @pl.when(t == 0)
         def _():
             raise_coefs(1)
+
+        pass_planes(f + 2, BOTH)
         take_rims(f + 2, BOTH)
-
-        def planes_both():
-            pass_planes(f + 2, BOTH)
-            take_corners(f + 2, BOTH)
-
-        apply(f + 2, f + 3, 1, BOTH, planes_both)
+        apply(f + 2, f + 3, 1, ((False, 1, True), (True, 0, False)), False)
+        take_corners(f + 2, BOTH)
+        apply(f + 2, f + 3, 1, ((False, 0, True), (True, 1, False)), True)
 
         settle(f, LOWER)
         settle(f + 1, UPPER)
@@ -474,7 +478,7 @@
         return carry
 
     lax.fori_loop(0, 2, round_body, 0)
-    for number in (3, 0, 1, 6, 7):
+    for number in (5, 0, 1, 10, 11):
         low_halo(number, "wait_send")
     gram(3, 5, 6)
 
@@ -522,7 +526,7 @@
     run(PLANE_PEERS, gather, "wait_send")
 
 
-def krylov(right_side, coefs):
+def krylov(right_side, *coefs):
     z_lo_count = lax.axis_size("group") // GROUP_Y
     z_hi_count = lax.axis_size("dev") // DEV_XC
     z_count = z_lo_count * z_hi_count
@@ -541,7 +545,7 @@
             jax.ShapeDtypeStruct(pieces, jnp.float32),
             jax.ShapeDtypeStruct((4, planes, comps, size, lanes), jnp.float32),
         ],
-        in_specs=[vmem] * 2,
+        in_specs=[vmem] * (1 + len(coefs)),
         out_specs=[vmem] * 2,
         scratch_shapes=[
             array(7, 4, comps, size, lanes),
@@ -562,25 +566,12 @@
         ],
         compiler_params=pltpu.CompilerParams(collective_id=0, has_side_effects=True),
         name="krylov",
-    )(right_side, coefs)
+    )(right_side, *coefs)
     return total.reshape(4 * size, size), vectors
 
 
-def per_device(right_side, stiff_diag, stiff_lower, fsai_diag, fsai_lower, fsai_pattern):
-    columns = right_side.shape[3]
-    lanes = stiff_diag.shape[3]
-    kept = fsai_pattern.astype(jnp.float32)
-    steps = jnp.array([c for _, _, c in lower_offsets])[:, None, None]
-    column = jnp.arange(lanes)[None, None, :] % columns + steps
-    inside = ((column >= 0) & (column < columns)).astype(jnp.float32)
-
-    def by_plane(diag, lower):
-        lower = (lower * inside).reshape((9,) + lower.shape[2:])
-        entries = jnp.concatenate([diag.reshape((9, 1) + diag.shape[2:]), lower], axis=1)
-        return jnp.transpose(entries, (2, 1, 0, 3))
-
-    coefs = jnp.stack([by_plane(fsai_diag, fsai_lower * kept[None, None]), by_plane(stiff_diag, stiff_lower)])
-    grams, basis = krylov(right_side, coefs)
+def per_device(right_side, *coefs):
+    grams, basis = krylov(right_side, *coefs)
     return finish(grams, right_side, basis)
 
 

time: 161 us -> 136 us (0.84)
  Pallas kernels: 155 us -> 135 us
  other arithmetic: 3.36 us -> 0 us
    pallas_call x1, Pallas kernels: 140 us -> 120 us  [krylov(): pl.pallas_call(functools.partial(krylov_kernel, z_lo_count, z_hi_count),...]
where the time goes in v3:
time: 136 us
  Pallas kernels  135 us (99%)
    pallas_call x1, Pallas kernels, krylov(): pl.pallas_call(functools.partial(krylov_kernel, z_lo_count, z_hi_count),...  120 us
    pallas_call x1, Pallas kernels, finish(): pl.pallas_call(finish_kernel, out_shape=[jax.ShapeDtypeStruct(right_side....  15.7 us

profile of v3, /device:TPU:1, one launch (start us, length us, event | category | flops | bytes accessed | tf_op | source)
XLA Modules:
  0.0 136.0 jit_solution(3474839767725474447)
XLA Ops:
  0.6 119.7 %krylov.1 = (f32[32,16,128]{2,1,0:T(8,128)}, f32[4,2,3,128,128]{4,3,2,1,0:T(8,128)}) custom-call(f32[3,2,2,64,128]{4,3,2,1,0:T(8,128)} %right_ref.3, f32[3,3,2,128]{3,2,1,0:T(2,128)} %stiff_diag_ref.1, f32[3,3,13,2,128]{4,3,2,1,0:T(2,128)} %stiff_ref.1, f32[3,3,2,128]{3,2,1,0:T(2,128)} %fsai_diag_ref.1, f32[3,3,13,2,128]{4,3,2,1,0:T(2,128)} %fsai_ref.1, ...), custom_call_target="tpu_custom_call" | custom-call | tf_op jit(solution)/shard_map/krylov/pallas_call | solution.py:542
  120.3 15.7 %finish.1 = (f32[3,2,2,64,128]{4,3,2,1,0:T(8,128)}, f32[3,2,2,64,128]{4,3,2,1,0:T(8,128)}) custom-call(f32[512,128]{1,0:T(8,128)} %bitcast.1, f32[3,2,2,64,128]{4,3,2,1,0:T(8,128)} %right_ref.3, f32[4,2,3,128,128]{4,3,2,1,0:T(8,128)} %get-tuple-element.5.basis_ref), custom_call_target="tpu_custom_call" | custom-call | tf_op jit(solution)/shard_map/finish/pallas_call | solution.py:115

commit v4 on v3

--- a/solution.py
+++ b/solution.py
@@ -79,12 +79,19 @@
 
 
 def finish_kernel(grams_ref, right_ref, basis_ref, solution_ref, residual_ref, scratch):
-    size = grams_ref.shape[1]
-    resid, energy, coupling, outer = [grams_ref[i * size : (i + 1) * size, :] for i in range(4)]
-    identity = (
-        lax.broadcasted_iota(jnp.int32, (size, size), 0) == lax.broadcasted_iota(jnp.int32, (size, size), 1)
-    ).astype(jnp.float32)
-    energy = 0.5 * (energy + energy.T)
+    size = grams_ref.shape[2]
+    row_id = lax.broadcasted_iota(jnp.int32, (size, size), 0)
+    column_id = lax.broadcasted_iota(jnp.int32, (size, size), 1)
+    identity = (row_id == column_id).astype(jnp.float32)
+    packed = grams_ref[:, :-1, :].reshape(2 * size, size)
+
+    def split(i):
+        pair, diag = packed[i * size : (i + 1) * size, :], grams_ref[i, -1:, :]
+        first = jnp.where(row_id >= column_id, pair, pair.T)
+        second = jnp.where(row_id < column_id, pair, pair.T)
+        return first, jnp.where(row_id == column_id, diag, second)
+
+    (resid, energy), (coupling, outer) = split(0), split(1)
     energy_inv, resid_inv = invert(scratch, energy, resid)
     step = mm(energy_inv, resid)
     shift = mm(energy, step)
@@ -117,21 +124,22 @@
             out_shape=[jax.ShapeDtypeStruct(right_side.shape, jnp.float32)] * 2,
             in_specs=[vmem] * 3,
             out_specs=[vmem] * 2,
-            scratch_shapes=[pltpu.VMEM((2, grams.shape[1], grams.shape[1]), jnp.float32)],
+            scratch_shapes=[pltpu.VMEM((2, grams.shape[2], grams.shape[2]), jnp.float32)],
             name="finish",
         )(grams, right_side, basis)
     )
 
 
-CHANNELS = 12
+CHANNELS = 8
 LOWER, UPPER, BOTH = 0, 1, 2
 SLOTS = len(lower_offsets)
-PHASES = 6
+PARTS = 2
+PHASES = 6 * PARTS
 
 
 def krylov_kernel(
     z_lo_count, z_hi_count, right_ref, stiff_diag_ref, stiff_ref, fsai_diag_ref, fsai_ref, kept_ref, total_ref, out_ref,
-    vec, edge, rim_out, rim_in, low, high, low_out, low_in, grams, rs_buf, z_buf,
+    vec, edge, rim_out, rim_in, low, high, low_out, low_in, mats, grams, rs_buf, z_buf,
     halo_send, halo_recv, send, recv, z_send, z_recv, a_send, a_recv,
 ):
     size, lanes = vec.shape[3:]
@@ -218,7 +226,9 @@
 
     for p in range(2):
         for c in range(3):
-            vec[0, p + 1, c] = right_ref[c, p].reshape(lanes, size).T
+            tile = right_ref[c, p].reshape(lanes, PARTS * size).T
+            for h in range(PARTS):
+                vec[h, p + 1, c] = tile[h * size : (h + 1) * size]
 
     left_low = left_of(low.shape[3:])
     left_half = left_of((size // 2, lanes))
@@ -249,10 +259,10 @@
         }
         if number < 2:
             return along[number]
-        if number < 8:
-            return along[2 if number < 5 else 3]
+        if number < 4:
+            return along[number]
         place, to, come = along[number % 2]
-        given = has_prev_group if number < 10 else has_next_group
+        given = has_prev_group if number < 6 else has_next_group
         return place, to & given, come & given
 
     def move(source, target, phase, number, method):
@@ -267,9 +277,9 @@
             )
             getattr(copy, method)()
 
-    def halo_plane(f, plane, c, method):
-        number, source = (2, 2) if plane == 0 else (5, 1)
-        move(vec.at[f, source, c], vec.at[f, plane, c], f, number + c, method)
+    def halo_plane(f, plane, method):
+        number, source = (2, 2) if plane == 0 else (3, 1)
+        move(vec.at[f, source], vec.at[f, plane], f, number, method)
 
     def halo_rim(f, side, kind, method):
         if side == 0:
@@ -278,16 +288,16 @@
             planes = pl.ds(1, 1) if kind == LOWER else pl.ds(1, 2)
         move(rim_out.at[f, side, planes], rim_in.at[f, side, planes], f, side, method)
 
-    def halo_corner(f, plane, side, method, comps=pl.ds(0, 3)):
-        number = (8 if plane == 0 else 10) + side
-        move(rim_out.at[f, side, plane, comps], rim_in.at[f, side, plane, comps], f, number, method)
+    def halo_corner(f, plane, side, method):
+        number = (4 if plane == 0 else 6) + side
+        move(rim_out.at[f, side, plane], rim_in.at[f, side, plane], f, number, method)
 
     def low_halo(number, method):
-        if number == 5:
+        if number == 3:
             move(low.at[:, 0], low.at[:, 2], PHASES, number, method)
             return
         side = number % 2
-        planes = pl.ds(2, 1) if number > 5 else (pl.ds(1, 1) if side == 0 else pl.ds(0, 2))
+        planes = pl.ds(2, 1) if number > 3 else (pl.ds(1, 1) if side == 0 else pl.ds(0, 2))
         move(low_out.at[side, planes], low_in.at[side, planes], PHASES, number, method)
 
     def pack(f, plane, c):
@@ -304,9 +314,8 @@
     outer_of = {LOWER: (0,), UPPER: (3,), BOTH: (0, 3)}
 
     def send_own(f, kind):
-        for c in range(3):
-            for plane in outer_of[kind]:
-                halo_plane(f, plane, c, "start")
+        for plane in outer_of[kind]:
+            halo_plane(f, plane, "start")
         for plane in (1, 2):
             for c in range(3):
                 pack(f, plane, c)
@@ -314,12 +323,12 @@
             halo_rim(f, side, kind, "start")
 
     def pass_planes(f, kind):
-        for c in range(3):
-            for plane in outer_of[kind]:
-                halo_plane(f, plane, c, "wait_recv")
+        for plane in outer_of[kind]:
+            halo_plane(f, plane, "wait_recv")
+            for c in range(3):
                 pack(f, plane, c)
-                for side in (0, 1):
-                    halo_corner(f, plane, side, "start", pl.ds(c, 1))
+            for side in (0, 1):
+                halo_corner(f, plane, side, "start")
 
     def take_rims(f, kind):
         for side in (0, 1):
@@ -339,8 +348,7 @@
             for plane in outer_of[kind]:
                 halo_corner(f, plane, side, "wait_send")
         for plane in outer_of[kind]:
-            for c in range(3):
-                halo_plane(f, plane, c, "wait_send")
+            halo_plane(f, plane, "wait_send")
 
     def raise_coefs(k):
         def body(p, carry):
@@ -408,79 +416,105 @@
                     vec[target, plane + 1, i, rows, :] = values[i]
             return carry
 
-        lax.fori_loop(0, size // rows_count, body, 0, unroll=2)
+        lax.fori_loop(0, size // rows_count, body, 0)
 
     def across(v):
-        return jnp.concatenate([vec[v, p, c] for p in (1, 2) for c in range(3)], axis=1)
+        parts = [
+            jnp.concatenate([vec[PARTS * v + h, p, c] for p in (1, 2) for c in range(3)], axis=1) for h in range(PARTS)
+        ]
+        return jnp.concatenate(parts, axis=0)
 
     def gram(index, v, w):
         one = across(v)
-        value = mm(one, one if w is None else across(w), ((1,), (1,)))
-        count = value.shape[0] // grams.shape[1]
-        grams[pl.ds(index * count, count)] = value.reshape((count,) + grams.shape[1:])
-
-    send_own(0, LOWER)
-    for number in (5, 0, 1):
+        mats[index] = mm(one, one if w is None else across(w), ((1,), (1,)))
+
+    def each_part(step):
+        def body(h, carry):
+            step(h)
+            return carry
+        lax.fori_loop(0, PARTS, body, 0)
+
+    def operate(v, k, kind, then):
+        early, late = {
+            LOWER: (((False, 1, True),), ((False, 0, True),)),
+            UPPER: (((True, 0, True),), ((True, 1, True),)),
+            BOTH: (((False, 1, True), (True, 0, False)), ((False, 0, True), (True, 1, False))),
+        }[kind]
+
+        def step(h):
+            f, target = PARTS * v + h, PARTS * (v + 1) + h
+            take_rims(f, kind)
+            apply(f, target, k, early, False)
+            take_corners(f, kind)
+            apply(f, target, k, late, kind == BOTH)
+            then(target)
+
+        each_part(step)
+
+    each_part(lambda h: send_own(h, LOWER))
+    for number in (3, 0, 1):
         low_halo(number, "start")
 
     def round_body(t, carry):
-        f = 3 * t
-
-        @pl.when(t == 1)
-        def _():
-            send_own(f, LOWER)
-            gram(1, 2, 3)
-
-        pass_planes(f, LOWER)
+        v = 3 * t
+        each_part(lambda h: pass_planes(PARTS * v + h, LOWER))
 
         @pl.when(t == 0)
         def _():
-            low_halo(5, "wait_recv")
+            low_halo(3, "wait_recv")
             pack_low(2)
-            for number in (10, 11):
+            for number in (6, 7):
                 low_halo(number, "start")
 
-        take_rims(f, LOWER)
-        apply(f, f + 1, 0, ((False, 1, True),), False)
-        take_corners(f, LOWER)
-        apply(f, f + 1, 0, ((False, 0, True),), False)
-
-        send_own(f + 1, UPPER)
-        gram(2 * t, f + 1, None)
+        operate(v, 0, LOWER, lambda f: send_own(f, UPPER))
+        gram(2 * t, v + 1, None)
 
         @pl.when(t == 0)
         def _():
-            for number in (0, 1, 10, 11):
+            for number in (0, 1, 6, 7):
                 low_halo(number, "wait_recv")
             raise_coefs(0)
 
-        pass_planes(f + 1, UPPER)
-        take_rims(f + 1, UPPER)
-        apply(f + 1, f + 2, 0, ((True, 0, True),), False)
-        take_corners(f + 1, UPPER)
-        apply(f + 1, f + 2, 0, ((True, 1, True),), False)
-
-        send_own(f + 2, BOTH)
+        each_part(lambda h: pass_planes(PARTS * (v + 1) + h, UPPER))
+        operate(v + 1, 0, UPPER, lambda f: send_own(f, BOTH))
 
         @pl.when(t == 0)
         def _():
             raise_coefs(1)
 
-        pass_planes(f + 2, BOTH)
-        take_rims(f + 2, BOTH)
-        apply(f + 2, f + 3, 1, ((False, 1, True), (True, 0, False)), False)
-        take_corners(f + 2, BOTH)
-        apply(f + 2, f + 3, 1, ((False, 0, True), (True, 1, False)), True)
-
-        settle(f, LOWER)
-        settle(f + 1, UPPER)
-        settle(f + 2, BOTH)
+        each_part(lambda h: pass_planes(PARTS * (v + 2) + h, BOTH))
+
+        def again(f):
+            @pl.when(t == 0)
+            def _():
+                send_own(f, LOWER)
+
+        operate(v + 2, 1, BOTH, again)
+        gram(2 * t + 1, v + 2, v + 3)
+
+        def settle_part(h):
+            settle(PARTS * v + h, LOWER)
+            settle(PARTS * (v + 1) + h, UPPER)
+            settle(PARTS * (v + 2) + h, BOTH)
+
+        each_part(settle_part)
         return carry
 
     lax.fori_loop(0, 2, round_body, 0)
-    for number in (5, 0, 1, 10, 11):
+    for number in (3, 0, 1, 6, 7):
         low_halo(number, "wait_send")
-    gram(3, 5, 6)
+
+    square = mats.shape[1:]
+    row_id = lax.broadcasted_iota(jnp.int32, square, 0)
+    column_id = lax.broadcasted_iota(jnp.int32, square, 1)
+    count = square[0] // (grams.shape[1] - 1)
+    grams[:, pl.ds(grams.shape[1] - 1, 1), :] = jnp.zeros((grams.shape[0], 1, square[1]), jnp.float32)
+    for i in range(2):
+        first, second = mats[2 * i], mats[2 * i + 1]
+        pair = jnp.where(row_id >= column_id, first, second)
+        grams[pl.ds(i * count, count), pl.ds(0, grams.shape[1] - 1), :] = pair.reshape(count, -1, square[1])
+        diag = jnp.sum(jnp.where(row_id == column_id, second, 0.0), axis=0, keepdims=True)
+        grams[i, pl.ds(grams.shape[1] - 1, 1), :] = diag
 
     def scatter(step):
         peer, place = plane_peer(step)
@@ -513,7 +547,8 @@
     rs_buf[me] = grams[me]
     for slot, v in enumerate((2, 3, 5, 6)):
         for p in range(2):
-            out_ref[slot, p] = vec[v, p + 1]
+            for h in range(PARTS):
+                out_ref[slot, p, :, pl.ds(h * size, size), :] = vec[PARTS * v + h, p + 1]
     run(PLANE_PEERS, scatter, "wait_recv")
     z_buf[my_z] = jnp.sum(rs_buf[...], axis=0)
     run(z_count, exchange, "start")
@@ -532,7 +567,8 @@
     z_count = z_lo_count * z_hi_count
     comps, planes, rows, columns, size = right_side.shape
     lanes = rows * columns
-    pieces = (PLANE_PEERS, 4 * size // PLANE_PEERS, size)
+    pieces = (PLANE_PEERS, 2 * size // PLANE_PEERS + 1, size)
+    part = size // PARTS
     vmem = pl.BlockSpec(memory_space=pltpu.VMEM)
     dma = pltpu.SemaphoreType.DMA
 
@@ -548,14 +584,15 @@
         in_specs=[vmem] * (1 + len(coefs)),
         out_specs=[vmem] * 2,
         scratch_shapes=[
-            array(7, 4, comps, size, lanes),
-            array(4, comps, size, lanes),
-            array(PHASES, 2, 4, comps, size // 2, lanes),
-            array(PHASES, 2, 4, comps, size // 2, lanes),
+            array(7 * PARTS, 4, comps, part, lanes),
+            array(4, comps, part, lanes),
+            array(PHASES, 2, 4, comps, part // 2, lanes),
+            array(PHASES, 2, 4, comps, part // 2, lanes),
             array(2, 3, SLOTS, 9, lanes),
             array(2, 2, SLOTS, 9, lanes),
             array(2, 3, SLOTS, 9, lanes),
             array(2, 3, SLOTS, 9, lanes),
+            array(4, size, size),
             array(*pieces),
             array(*pieces),
             array(z_count, *pieces[1:]),
@@ -567,7 +604,7 @@
         compiler_params=pltpu.CompilerParams(collective_id=0, has_side_effects=True),
         name="krylov",
     )(right_side, *coefs)
-    return total.reshape(4 * size, size), vectors
+    return total, vectors
 
 
 def per_device(right_side, *coefs):

time: 136 us -> 127 us (0.934)
  Pallas kernels: 135 us -> 126 us
    pallas_call x1, Pallas kernels: 120 us -> 111 us  [krylov(): pl.pallas_call(functools.partial(krylov_kernel, z_lo_count, z_hi_count),...]
where the time goes in v4:
time: 127 us
  Pallas kernels  126 us (99%)
    pallas_call x1, Pallas kernels, krylov(): pl.pallas_call(functools.partial(krylov_kernel, z_lo_count, z_hi_count),...  111 us
    pallas_call x1, Pallas kernels, finish(): pl.pallas_call(finish_kernel, out_shape=[jax.ShapeDtypeStruct(right_side....  15.7 us

profile of v4, /device:TPU:1, one launch (start us, length us, event | category | flops | bytes accessed | tf_op | source)
XLA Modules:
  0.0 127.0 jit_solution(7232827582132497447)
XLA Ops:
  0.6 110.7 %krylov.1 = (f32[32,9,128]{2,1,0:T(8,128)}, f32[4,2,3,128,128]{4,3,2,1,0:T(8,128)}) custom-call(f32[3,2,2,64,128]{4,3,2,1,0:T(8,128)} %right_ref.3, f32[3,3,2,128]{3,2,1,0:T(2,128)} %stiff_diag_ref.1, f32[3,3,13,2,128]{4,3,2,1,0:T(2,128)} %stiff_ref.1, f32[3,3,2,128]{3,2,1,0:T(2,128)} %fsai_diag_ref.1, f32[3,3,13,2,128]{4,3,2,1,0:T(2,128)} %fsai_ref.1, ...), custom_call_target="tpu_custom_call" | custom-call | tf_op jit(solution)/shard_map/krylov/pallas_call | solution.py:578
  111.3 15.7 %finish.1 = (f32[3,2,2,64,128]{4,3,2,1,0:T(8,128)}, f32[3,2,2,64,128]{4,3,2,1,0:T(8,128)}) custom-call(f32[32,9,128]{2,1,0:T(8,128)} %get-tuple-element.4.grams_ref, f32[3,2,2,64,128]{4,3,2,1,0:T(8,128)} %right_ref.3, f32[4,2,3,128,128]{4,3,2,1,0:T(8,128)} %get-tuple-element.5.basis_ref), custom_call_target="tpu_custom_call" | custom-call | tf_op jit(solution)/shard_map/finish/pallas_call | solution.py:122

commit v5 on v4

--- a/solution.py
+++ b/solution.py
@@ -78,7 +78,16 @@
     return [scratch[i] * down * across for i, (down, across) in enumerate(scales)]
 
 
-def finish_kernel(grams_ref, right_ref, basis_ref, solution_ref, residual_ref, scratch):
+def finish_kernel(
+    grams_ref, right_hbm, basis_hbm, solution_hbm, residual_hbm, scratch, right_ref, basis_ref, solution_ref, residual_ref,
+    in_sem, out_sem,
+):
+    loads = [
+        pltpu.make_async_copy(basis_hbm, basis_ref, in_sem.at[0]),
+        pltpu.make_async_copy(right_hbm, right_ref, in_sem.at[1]),
+    ]
+    for load in loads:
+        load.start()
     size = grams_ref.shape[2]
     row_id = lax.broadcasted_iota(jnp.int32, (size, size), 0)
     column_id = lax.broadcasted_iota(jnp.int32, (size, size), 1)
@@ -106,31 +115,44 @@
     near = step + mm(grow, next_step)
     far = mm(step, next_step)
     weights = jnp.concatenate([near.T, -far.T], axis=1)
-    planes, comps = basis_ref.shape[1:3]
-    for p in range(planes):
-        for c in range(comps):
+    for load in loads:
+        load.wait()
+    parts, planes, comps = basis_ref.shape[1:4]
+    stores = []
+    for c in range(comps):
+        for p in range(planes):
             block = right_ref.shape[2:]
-            ahead = mm(weights, jnp.concatenate([basis_ref[0, p, c], basis_ref[2, p, c]]))
-            drop = mm(weights, jnp.concatenate([basis_ref[1, p, c], basis_ref[3, p, c]]))
-            solution_ref[c, p] = ahead.T.reshape(block)
-            residual_ref[c, p] = right_ref[c, p] - drop.T.reshape(block)
+
+            def pair(one, other):
+                return jnp.concatenate([basis_ref[slot, h, p, c] for slot in (one, other) for h in range(parts)])
+
+            solution_ref[c, p] = mm(weights, pair(0, 2)).T.reshape(block)
+            residual_ref[c, p] = right_ref[c, p] - mm(weights, pair(1, 3)).T.reshape(block)
+        for k, (source, target) in enumerate(((solution_ref, solution_hbm), (residual_ref, residual_hbm))):
+            stores.append(pltpu.make_async_copy(source.at[c], target.at[c], out_sem.at[k, c]))
+            stores[-1].start()
+    for store in stores:
+        store.wait()
 
 
 def finish(grams, right_side, basis):
-    vmem = pl.BlockSpec(memory_space=pltpu.VMEM)
+    vmem, whole = pl.BlockSpec(memory_space=pltpu.VMEM), pl.BlockSpec(memory_space=pl.ANY)
+    size = grams.shape[2]
+    scratch_of = [(2, size, size), right_side.shape, basis.shape, right_side.shape, right_side.shape]
     return tuple(
         pl.pallas_call(
             finish_kernel,
             out_shape=[jax.ShapeDtypeStruct(right_side.shape, jnp.float32)] * 2,
-            in_specs=[vmem] * 3,
-            out_specs=[vmem] * 2,
-            scratch_shapes=[pltpu.VMEM((2, grams.shape[2], grams.shape[2]), jnp.float32)],
+            in_specs=[vmem, whole, whole],
+            out_specs=[whole] * 2,
+            scratch_shapes=[pltpu.VMEM(shape, jnp.float32) for shape in scratch_of]
+            + [pltpu.SemaphoreType.DMA((2,)), pltpu.SemaphoreType.DMA((2, right_side.shape[0]))],
             name="finish",
         )(grams, right_side, basis)
     )
 
 
-CHANNELS = 8
+CHANNELS = 12
 LOWER, UPPER, BOTH = 0, 1, 2
 SLOTS = len(lower_offsets)
 PARTS = 2
@@ -140,7 +162,7 @@
 def krylov_kernel(
     z_lo_count, z_hi_count, right_ref, stiff_diag_ref, stiff_ref, fsai_diag_ref, fsai_ref, kept_ref, total_ref, out_ref,
     vec, edge, rim_out, rim_in, low, high, low_out, low_in, mats, grams, rs_buf, z_buf,
-    halo_send, halo_recv, send, recv, z_send, z_recv, a_send, a_recv,
+    halo_send, halo_recv, send, recv, z_send, z_recv, a_send, a_recv, out_sem,
 ):
     size, lanes = vec.shape[3:]
     half, top, bottom = lanes // 2, pl.ds(0, size // 2), pl.ds(size // 2, size // 2)
@@ -153,6 +175,7 @@
     z_count = z_lo_count * z_hi_count
     has_prev_dev, has_next_dev = dev > 0, dev < dev_count - 1
     has_prev_group, has_next_group = group > 0, group < group_count - 1
+    near_prev, near_next = dev % DEV_XC > 0, dev % DEV_XC < DEV_XC - 1
     prev_dev, next_dev = (group, dev - 1), (group, dev + 1)
     prev_group, next_group = (group - 1, dev), (group + 1, dev)
 
@@ -250,7 +273,7 @@
         pack_low(p)
     pl.semaphore_wait(barrier, PLANE_PEERS - 1 + z_count - 1 + len(neighbours))
 
-    def route(number):
+    def route(number, own_way):
         along = {
             0: (next_dev, has_next_dev, has_prev_dev),
             1: (prev_dev, has_prev_dev, has_next_dev),
@@ -263,10 +286,12 @@
             return along[number]
         place, to, come = along[number % 2]
         given = has_prev_group if number < 6 else has_next_group
+        if own_way:
+            to = to & (near_next if number % 2 == 0 else near_prev)
         return place, to & given, come & given
 
-    def move(source, target, phase, number, method):
-        place, to, come = route(number)
+    def move(source, target, phase, number, method, own_way=False):
+        place, to, come = route(number, own_way)
 
         @pl.when(come if method == "wait_recv" else to)
         def _():
@@ -281,16 +306,26 @@
         number, source = (2, 2) if plane == 0 else (3, 1)
         move(vec.at[f, source], vec.at[f, plane], f, number, method)
 
-    def halo_rim(f, side, kind, method):
-        if side == 0:
-            planes = pl.ds(2, 1) if kind == UPPER else pl.ds(1, 2)
-        else:
-            planes = pl.ds(1, 1) if kind == LOWER else pl.ds(1, 2)
-        move(rim_out.at[f, side, planes], rim_in.at[f, side, planes], f, side, method)
+    def halo_rim(f, side, method):
+        move(rim_out.at[f, side, pl.ds(1, 2)], rim_in.at[f, side, pl.ds(1, 2)], f, side, method)
 
     def halo_corner(f, plane, side, method):
         number = (4 if plane == 0 else 6) + side
-        move(rim_out.at[f, side, plane], rim_in.at[f, side, plane], f, number, method)
+        move(rim_out.at[f, side, plane], rim_in.at[f, side, plane], f, number, method, True)
+
+    def far_corner(f, plane, side, method):
+        place, exists = (next_group, has_next_group) if plane == 0 else (prev_group, has_prev_group)
+        far = has_prev_dev & jnp.logical_not(near_prev) if side == 0 else has_next_dev & jnp.logical_not(near_next)
+        number = (4 if plane == 0 else 6) + side
+
+        @pl.when(exists & far)
+        def _():
+            copy = pltpu.make_async_remote_copy(
+                src_ref=rim_in.at[f, side, 2 if plane == 0 else 1], dst_ref=rim_in.at[f, side, plane],
+                send_sem=halo_send.at[f, number + 4], recv_sem=halo_recv.at[f, number],
+                device_id=place, device_id_type=MESH,
+            )
+            getattr(copy, method)()
 
     def low_halo(number, method):
         if number == 3:
@@ -320,7 +355,7 @@
             for c in range(3):
                 pack(f, plane, c)
         for side in (0, 1):
-            halo_rim(f, side, kind, "start")
+            halo_rim(f, side, "start")
 
     def pass_planes(f, kind):
         for plane in outer_of[kind]:
@@ -329,10 +364,12 @@
                 pack(f, plane, c)
             for side in (0, 1):
                 halo_corner(f, plane, side, "start")
-
-    def take_rims(f, kind):
         for side in (0, 1):
-            halo_rim(f, side, kind, "wait_recv")
+            halo_rim(f, side, "wait_recv")
+            for plane in outer_of[kind]:
+                far_corner(f, plane, side, "start")
+
+    def take_rims(f):
         for plane in (1, 2):
             unpack(f, plane)
 
@@ -344,9 +381,10 @@
 
     def settle(f, kind):
         for side in (0, 1):
-            halo_rim(f, side, kind, "wait_send")
+            halo_rim(f, side, "wait_send")
             for plane in outer_of[kind]:
                 halo_corner(f, plane, side, "wait_send")
+                far_corner(f, plane, side, "wait_send")
         for plane in outer_of[kind]:
             halo_plane(f, plane, "wait_send")
 
@@ -428,6 +466,9 @@
         one = across(v)
         mats[index] = mm(one, one if w is None else across(w), ((1,), (1,)))
 
+    def emit(slot, v):
+        return pltpu.make_async_copy(vec.at[pl.ds(PARTS * v, PARTS), pl.ds(1, 2)], out_ref.at[slot], out_sem.at[slot])
+
     def each_part(step):
         def body(h, carry):
             step(h)
@@ -443,7 +484,7 @@
 
         def step(h):
             f, target = PARTS * v + h, PARTS * (v + 1) + h
-            take_rims(f, kind)
+            take_rims(f)
             apply(f, target, k, early, False)
             take_corners(f, kind)
             apply(f, target, k, late, kind == BOTH)
@@ -477,6 +518,7 @@
 
         each_part(lambda h: pass_planes(PARTS * (v + 1) + h, UPPER))
         operate(v + 1, 0, UPPER, lambda f: send_own(f, BOTH))
+        emit(2 * t, v + 2).start()
 
         @pl.when(t == 0)
         def _():
@@ -490,6 +532,7 @@
                 send_own(f, LOWER)
 
         operate(v + 2, 1, BOTH, again)
+        emit(2 * t + 1, v + 3).start()
         gram(2 * t + 1, v + 2, v + 3)
 
         def settle_part(h):
@@ -545,10 +588,6 @@
 
     run(PLANE_PEERS, scatter, "start")
     rs_buf[me] = grams[me]
-    for slot, v in enumerate((2, 3, 5, 6)):
-        for p in range(2):
-            for h in range(PARTS):
-                out_ref[slot, p, :, pl.ds(h * size, size), :] = vec[PARTS * v + h, p + 1]
     run(PLANE_PEERS, scatter, "wait_recv")
     z_buf[my_z] = jnp.sum(rs_buf[...], axis=0)
     run(z_count, exchange, "start")
@@ -559,6 +598,8 @@
     run(PLANE_PEERS, scatter, "wait_send")
     run(z_count, exchange, "wait_send")
     run(PLANE_PEERS, gather, "wait_send")
+    for slot, v in enumerate((2, 3, 5, 6)):
+        emit(slot, v).wait()
 
 
 def krylov(right_side, *coefs):
@@ -579,10 +620,10 @@
         functools.partial(krylov_kernel, z_lo_count, z_hi_count),
         out_shape=[
             jax.ShapeDtypeStruct(pieces, jnp.float32),
-            jax.ShapeDtypeStruct((4, planes, comps, size, lanes), jnp.float32),
+            jax.ShapeDtypeStruct((4, PARTS, planes, comps, part, lanes), jnp.float32),
         ],
         in_specs=[vmem] * (1 + len(coefs)),
-        out_specs=[vmem] * 2,
+        out_specs=[vmem, pl.BlockSpec(memory_space=pl.ANY)],
         scratch_shapes=[
             array(7 * PARTS, 4, comps, part, lanes),
             array(4, comps, part, lanes),
@@ -600,6 +641,7 @@
             dma((PLANE_PEERS,)), dma((PLANE_PEERS,)),
             dma((z_count,)), dma((z_count,)),
             dma((PLANE_PEERS,)), dma((PLANE_PEERS,)),
+            dma((4,)),
         ],
         compiler_params=pltpu.CompilerParams(collective_id=0, has_side_effects=True),
         name="krylov",

time: 127 us -> 127 us (level)
  no operation moved by 1% of the time
where the time goes in v5:
time: 127 us
  Pallas kernels  126 us (99%)
    pallas_call x1, Pallas kernels, krylov(): pl.pallas_call(functools.partial(krylov_kernel, z_lo_count, z_hi_count),...  111 us
    pallas_call x1, Pallas kernels, finish(): pl.pallas_call(finish_kernel, out_shape=[jax.ShapeDtypeStruct(right_side....  15 us

profile of v5, /device:TPU:1, one launch (start us, length us, event | category | flops | bytes accessed | tf_op | source)
XLA Modules:
  0.0 127.1 jit_solution(7360604341933832764)
XLA Ops:
  0.6 111.5 %krylov.1 = (f32[32,9,128]{2,1,0:T(8,128)}, f32[4,2,2,3,64,128]{5,4,3,2,1,0:T(8,128)}) custom-call(f32[3,2,2,64,128]{4,3,2,1,0:T(8,128)} %right_hbm.1, f32[3,3,2,128]{3,2,1,0:T(2,128)} %stiff_diag_ref.1, f32[3,3,13,2,128]{4,3,2,1,0:T(2,128)} %stiff_ref.1, f32[3,3,2,128]{3,2,1,0:T(2,128)} %fsai_diag_ref.1, f32[3,3,13,2,128]{4,3,2,1,0:T(2,128)} %fsai_ref.1, ...), custom_call_target="tpu_custom_call" | custom-call | tf_op jit(solution)/shard_map/krylov/pallas_call | solution.py:619
  112.1 15.0 %finish.1 = (f32[3,2,2,64,128]{4,3,2,1,0:T(8,128)}, f32[3,2,2,64,128]{4,3,2,1,0:T(8,128)}) custom-call(f32[32,9,128]{2,1,0:T(8,128)} %get-tuple-element.4.grams_ref, f32[3,2,2,64,128]{4,3,2,1,0:T(8,128)} %right_hbm.1, f32[4,2,2,3,64,128]{5,4,3,2,1,0:T(8,128)} %get-tuple-element.5.basis_hbm), custom_call_target="tpu_custom_call" | custom-call | tf_op jit(solution)/shard_map/finish/pallas_call | solution.py:143

commit v6 on v5

--- a/solution.py
+++ b/solution.py
@@ -22,6 +22,16 @@
 
 
 TRANS = ((0,), (0,))
+
+
+def halves(value):
+    high = value.astype(jnp.bfloat16)
+    return high, (value - high.astype(jnp.float32)).astype(jnp.bfloat16)
+
+
+def mm_halves(left, right):
+    (a, b), (c, d) = left, halves(right)
+    return sum(jnp.dot(x, y, preferred_element_type=jnp.float32) for x, y in ((a, d), (b, c), (a, c)))
 
 
 def sweep(matrix, row_id, column_id):
@@ -114,7 +124,7 @@
     next_step = mm(next_inv, next_gram)
     near = step + mm(grow, next_step)
     far = mm(step, next_step)
-    weights = jnp.concatenate([near.T, -far.T], axis=1)
+    weights = halves(jnp.concatenate([near.T, -far.T], axis=1))
     for load in loads:
         load.wait()
     parts, planes, comps = basis_ref.shape[1:4]
@@ -126,8 +136,8 @@
             def pair(one, other):
                 return jnp.concatenate([basis_ref[slot, h, p, c] for slot in (one, other) for h in range(parts)])
 
-            solution_ref[c, p] = mm(weights, pair(0, 2)).T.reshape(block)
-            residual_ref[c, p] = right_ref[c, p] - mm(weights, pair(1, 3)).T.reshape(block)
+            solution_ref[c, p] = mm_halves(weights, pair(0, 2)).T.reshape(block)
+            residual_ref[c, p] = right_ref[c, p] - mm_halves(weights, pair(1, 3)).T.reshape(block)
         for k, (source, target) in enumerate(((solution_ref, solution_hbm), (residual_ref, residual_hbm))):
             stores.append(pltpu.make_async_copy(source.at[c], target.at[c], out_sem.at[k, c]))
             stores[-1].start()
@@ -155,7 +165,7 @@
 CHANNELS = 12
 LOWER, UPPER, BOTH = 0, 1, 2
 SLOTS = len(lower_offsets)
-PARTS = 2
+PARTS = 4
 PHASES = 6 * PARTS
 
 
@@ -229,10 +239,9 @@
             return carry
         lax.fori_loop(1, count, body, 0)
 
-    neighbours = (
-        (group, (dev + dev_count - 1) % dev_count), (group, (dev + 1) % dev_count),
-        ((group + group_count - 1) % group_count, dev), ((group + 1) % group_count, dev),
-    )
+    around = [(1, 0), (dev_count - 1, 0), (0, 1), (0, group_count - 1)]
+    around += [(a, b) for a in (1, dev_count - 1) for b in (1, group_count - 1)]
+    neighbours = [((group + b) % group_count, (dev + a) % dev_count) for a, b in around]
     greet_all(PLANE_PEERS, plane_peer)
     greet_all(z_count, z_peer)
     for place in neighbours:
@@ -306,24 +315,28 @@
         number, source = (2, 2) if plane == 0 else (3, 1)
         move(vec.at[f, source], vec.at[f, plane], f, number, method)
 
-    def halo_rim(f, side, method):
-        move(rim_out.at[f, side, pl.ds(1, 2)], rim_in.at[f, side, pl.ds(1, 2)], f, side, method)
+    def halo_rim(f, side, kind, method):
+        if side == 0:
+            planes = pl.ds(2, 1) if kind == UPPER else pl.ds(1, 2)
+        else:
+            planes = pl.ds(1, 1) if kind == LOWER else pl.ds(1, 2)
+        move(rim_out.at[f, side, planes], rim_in.at[f, side, planes], f, side, method)
 
     def halo_corner(f, plane, side, method):
         number = (4 if plane == 0 else 6) + side
         move(rim_out.at[f, side, plane], rim_in.at[f, side, plane], f, number, method, True)
 
     def far_corner(f, plane, side, method):
-        place, exists = (next_group, has_next_group) if plane == 0 else (prev_group, has_prev_group)
-        far = has_prev_dev & jnp.logical_not(near_prev) if side == 0 else has_next_dev & jnp.logical_not(near_next)
+        ahead, on = (1, has_next_group) if plane == 0 else (-1, has_prev_group)
+        far = has_next_dev & jnp.logical_not(near_next) if side == 0 else has_prev_dev & jnp.logical_not(near_prev)
         number = (4 if plane == 0 else 6) + side
 
-        @pl.when(exists & far)
+        @pl.when(on & far)
         def _():
             copy = pltpu.make_async_remote_copy(
-                src_ref=rim_in.at[f, side, 2 if plane == 0 else 1], dst_ref=rim_in.at[f, side, plane],
+                src_ref=rim_out.at[f, side, 2 if plane == 0 else 1], dst_ref=rim_in.at[f, side, plane],
                 send_sem=halo_send.at[f, number + 4], recv_sem=halo_recv.at[f, number],
-                device_id=place, device_id_type=MESH,
+                device_id=(group + ahead, dev + (1 if side == 0 else -1)), device_id_type=MESH,
             )
             getattr(copy, method)()
 
@@ -355,7 +368,9 @@
             for c in range(3):
                 pack(f, plane, c)
         for side in (0, 1):
-            halo_rim(f, side, "start")
+            halo_rim(f, side, kind, "start")
+            for plane in outer_of[kind]:
+                far_corner(f, plane, side, "start")
 
     def pass_planes(f, kind):
         for plane in outer_of[kind]:
@@ -364,12 +379,10 @@
                 pack(f, plane, c)
             for side in (0, 1):
                 halo_corner(f, plane, side, "start")
+
+    def take_rims(f, kind):
         for side in (0, 1):
-            halo_rim(f, side, "wait_recv")
-            for plane in outer_of[kind]:
-                far_corner(f, plane, side, "start")
-
-    def take_rims(f):
+            halo_rim(f, side, kind, "wait_recv")
         for plane in (1, 2):
             unpack(f, plane)
 
@@ -381,7 +394,7 @@
 
     def settle(f, kind):
         for side in (0, 1):
-            halo_rim(f, side, "wait_send")
+            halo_rim(f, side, kind, "wait_send")
             for plane in outer_of[kind]:
                 halo_corner(f, plane, side, "wait_send")
                 far_corner(f, plane, side, "wait_send")
@@ -484,7 +497,12 @@
 
         def step(h):
             f, target = PARTS * v + h, PARTS * (v + 1) + h
-            take_rims(f)
+
+            @pl.when(h < PARTS - 1)
+            def _():
+                pass_planes(f + 1, kind)
+
+            take_rims(f, kind)
             apply(f, target, k, early, False)
             take_corners(f, kind)
             apply(f, target, k, late, kind == BOTH)
@@ -498,7 +516,7 @@
 
     def round_body(t, carry):
         v = 3 * t
-        each_part(lambda h: pass_planes(PARTS * v + h, LOWER))
+        pass_planes(PARTS * v, LOWER)
 
         @pl.when(t == 0)
         def _():
@@ -516,7 +534,7 @@
                 low_halo(number, "wait_recv")
             raise_coefs(0)
 
-        each_part(lambda h: pass_planes(PARTS * (v + 1) + h, UPPER))
+        pass_planes(PARTS * (v + 1), UPPER)
         operate(v + 1, 0, UPPER, lambda f: send_own(f, BOTH))
         emit(2 * t, v + 2).start()
 
@@ -524,7 +542,7 @@
         def _():
             raise_coefs(1)
 
-        each_part(lambda h: pass_planes(PARTS * (v + 2) + h, BOTH))
+        pass_planes(PARTS * (v + 2), BOTH)
 
         def again(f):
             @pl.when(t == 0)
@@ -534,19 +552,9 @@
         operate(v + 2, 1, BOTH, again)
         emit(2 * t + 1, v + 3).start()
         gram(2 * t + 1, v + 2, v + 3)
-
-        def settle_part(h):
-            settle(PARTS * v + h, LOWER)
-            settle(PARTS * (v + 1) + h, UPPER)
-            settle(PARTS * (v + 2) + h, BOTH)
-
-        each_part(settle_part)
         return carry
 
     lax.fori_loop(0, 2, round_body, 0)
-    for number in (3, 0, 1, 6, 7):
-        low_halo(number, "wait_send")
-
     square = mats.shape[1:]
     row_id = lax.broadcasted_iota(jnp.int32, square, 0)
     column_id = lax.broadcasted_iota(jnp.int32, square, 1)
@@ -588,18 +596,30 @@
 
     run(PLANE_PEERS, scatter, "start")
     rs_buf[me] = grams[me]
+
+    def settle_round(t, carry):
+        def settle_part(h):
+            for k, kind in enumerate((LOWER, UPPER, BOTH)):
+                settle(PARTS * (3 * t + k) + h, kind)
+
+        each_part(settle_part)
+        return carry
+
+    lax.fori_loop(0, 2, settle_round, 0)
+    for number in (3, 0, 1, 6, 7):
+        low_halo(number, "wait_send")
     run(PLANE_PEERS, scatter, "wait_recv")
     z_buf[my_z] = jnp.sum(rs_buf[...], axis=0)
     run(z_count, exchange, "start")
+    run(PLANE_PEERS, scatter, "wait_send")
     run(z_count, exchange, "wait_recv")
     total_ref[me] = jnp.sum(z_buf[...], axis=0)
     run(PLANE_PEERS, gather, "start")
-    run(PLANE_PEERS, gather, "wait_recv")
-    run(PLANE_PEERS, scatter, "wait_send")
     run(z_count, exchange, "wait_send")
-    run(PLANE_PEERS, gather, "wait_send")
     for slot, v in enumerate((2, 3, 5, 6)):
         emit(slot, v).wait()
+    run(PLANE_PEERS, gather, "wait_recv")
+    run(PLANE_PEERS, gather, "wait_send")
 
 
 def krylov(right_side, *coefs):

time: 127 us -> 123 us (0.969)
  Pallas kernels: 126 us -> 123 us
    pallas_call x1, Pallas kernels: 111 us -> 108 us  [krylov(): pl.pallas_call(functools.partial(krylov_kernel, z_lo_count, z_hi_count),...]
where the time goes in v6:
time: 123 us
  Pallas kernels  123 us (100%)
    pallas_call x1, Pallas kernels, krylov(): pl.pallas_call(functools.partial(krylov_kernel, z_lo_count, z_hi_count),...  108 us
    pallas_call x1, Pallas kernels, finish(): pl.pallas_call(finish_kernel, out_shape=[jax.ShapeDtypeStruct(right_side....  14.3 us

profile of v6, /device:TPU:1, one launch (start us, length us, event | category | flops | bytes accessed | tf_op | source)
XLA Modules:
  0.0 123.3 jit_solution(9709343652416894838)
XLA Ops:
  0.6 108.3 %krylov.1 = (f32[32,9,128]{2,1,0:T(8,128)}, f32[4,4,2,3,32,128]{5,4,3,2,1,0:T(8,128)}) custom-call(f32[3,2,2,64,128]{4,3,2,1,0:T(8,128)} %right_hbm.1, f32[3,3,2,128]{3,2,1,0:T(2,128)} %stiff_diag_ref.1, f32[3,3,13,2,128]{4,3,2,1,0:T(2,128)} %stiff_ref.1, f32[3,3,2,128]{3,2,1,0:T(2,128)} %fsai_diag_ref.1, f32[3,3,13,2,128]{4,3,2,1,0:T(2,128)} %fsai_ref.1, ...), custom_call_target="tpu_custom_call" | custom-call | tf_op jit(solution)/shard_map/krylov/pallas_call | solution.py:639
  108.9 14.3 %finish.1 = (f32[3,2,2,64,128]{4,3,2,1,0:T(8,128)}, f32[3,2,2,64,128]{4,3,2,1,0:T(8,128)}) custom-call(f32[32,9,128]{2,1,0:T(8,128)} %get-tuple-element.4.grams_ref, f32[3,2,2,64,128]{4,3,2,1,0:T(8,128)} %right_hbm.1, f32[4,4,2,3,32,128]{5,4,3,2,1,0:T(8,128)} %get-tuple-element.5.basis_hbm), custom_call_target="tpu_custom_call" | custom-call | tf_op jit(solution)/shard_map/finish/pallas_call | solution.py:153

commit v7 on v6

--- a/solution.py
+++ b/solution.py
@@ -67,20 +67,20 @@
 
     def more(state):
         count, error = state
-        return (error > 1e-8) & (count < 16)
+        return (error > 1e-7) & (count < 16)
 
     def newton(state):
         error = 0.0
         for i, unit in enumerate(scaled):
             guess = scratch[i]
             miss = identity - mm(unit, guess)
-            scratch[i] = guess + mm(guess, miss)
+            scratch[i] = guess + mm_halves(halves(guess), miss)
             error = jnp.maximum(error, jnp.sum(miss * miss))
         return state[0] + 1, error
 
     _, error = lax.while_loop(more, newton, (0, jnp.float32(1.0)))
 
-    @pl.when(jnp.logical_not(error <= 1e-8))
+    @pl.when(jnp.logical_not(error <= 1e-7))
     def _():
         for i, unit in enumerate(scaled):
             scratch[i] = sweep(unit, row_id, column_id)
@@ -190,12 +190,12 @@
     prev_group, next_group = (group - 1, dev), (group + 1, dev)
 
     def plane_peer(step):
-        peer = (me + step) % PLANE_PEERS
-        return peer, (z_lo * GROUP_Y + peer // DEV_XC, z_hi * DEV_XC + peer % DEV_XC)
+        peer = lax.rem(me + step, PLANE_PEERS)
+        return peer, (z_lo * GROUP_Y + lax.div(peer, DEV_XC), z_hi * DEV_XC + lax.rem(peer, DEV_XC))
 
     def z_peer(step):
-        peer = (my_z + step) % z_count
-        return peer, (peer % z_lo_count * GROUP_Y + y, peer // z_lo_count * DEV_XC + xc)
+        peer = lax.rem(my_z + step, z_count)
+        return peer, (lax.rem(peer, z_lo_count) * GROUP_Y + y, lax.div(peer, z_lo_count) * DEV_XC + xc)
 
     def clear(ref):
         ref[...] = jnp.zeros(ref.shape, ref.dtype)
@@ -237,7 +237,7 @@
         def body(step, carry):
             greet(peer_of(step)[1])
             return carry
-        lax.fori_loop(1, count, body, 0)
+        lax.fori_loop(1, count, body, 0, unroll=True)
 
     around = [(1, 0), (dev_count - 1, 0), (0, 1), (0, group_count - 1)]
     around += [(a, b) for a in (1, dev_count - 1) for b in (1, group_count - 1)]
@@ -592,7 +592,7 @@
         def body(step, carry):
             getattr(make(step), method)()
             return carry
-        lax.fori_loop(1, count, body, 0)
+        lax.fori_loop(1, count, body, 0, unroll=method != "wait_send")
 
     run(PLANE_PEERS, scatter, "start")
     rs_buf[me] = grams[me]

time: 123 us -> 126 us (1.024)
  Pallas kernels: 123 us -> 125 us
    pallas_call x1, Pallas kernels: 108 us -> 110 us  [krylov(): pl.pallas_call(functools.partial(krylov_kernel, z_lo_count, z_hi_count),...]
where the time goes in v7:
time: 126 us
  Pallas kernels  125 us (99%)
    pallas_call x1, Pallas kernels, krylov(): pl.pallas_call(functools.partial(krylov_kernel, z_lo_count, z_hi_count),...  110 us
    pallas_call x1, Pallas kernels, finish(): pl.pallas_call(finish_kernel, out_shape=[jax.ShapeDtypeStruct(right_side....  15 us

profile of v7, /device:TPU:1, one launch (start us, length us, event | category | flops | bytes accessed | tf_op | source)
XLA Modules:
  0.0 125.8 jit_solution(1768503087844652244)
XLA Ops:
  0.6 110.2 %krylov.1 = (f32[32,9,128]{2,1,0:T(8,128)}, f32[4,4,2,3,32,128]{5,4,3,2,1,0:T(8,128)}) custom-call(f32[3,2,2,64,128]{4,3,2,1,0:T(8,128)} %right_hbm.1, f32[3,3,2,128]{3,2,1,0:T(2,128)} %stiff_diag_ref.1, f32[3,3,13,2,128]{4,3,2,1,0:T(2,128)} %stiff_ref.1, f32[3,3,2,128]{3,2,1,0:T(2,128)} %fsai_diag_ref.1, f32[3,3,13,2,128]{4,3,2,1,0:T(2,128)} %fsai_ref.1, ...), custom_call_target="tpu_custom_call" | custom-call | tf_op jit(solution)/shard_map/krylov/pallas_call | solution.py:639
  110.8 15.0 %finish.1 = (f32[3,2,2,64,128]{4,3,2,1,0:T(8,128)}, f32[3,2,2,64,128]{4,3,2,1,0:T(8,128)}) custom-call(f32[32,9,128]{2,1,0:T(8,128)} %get-tuple-element.4.grams_ref, f32[3,2,2,64,128]{4,3,2,1,0:T(8,128)} %right_hbm.1, f32[4,4,2,3,32,128]{5,4,3,2,1,0:T(8,128)} %get-tuple-element.5.basis_hbm), custom_call_target="tpu_custom_call" | custom-call | tf_op jit(solution)/shard_map/finish/pallas_call | solution.py:153

commit v8 on v7

--- a/solution.py
+++ b/solution.py
@@ -237,7 +237,7 @@
         def body(step, carry):
             greet(peer_of(step)[1])
             return carry
-        lax.fori_loop(1, count, body, 0, unroll=True)
+        lax.fori_loop(1, count, body, 0)
 
     around = [(1, 0), (dev_count - 1, 0), (0, 1), (0, group_count - 1)]
     around += [(a, b) for a in (1, dev_count - 1) for b in (1, group_count - 1)]
@@ -592,7 +592,7 @@
         def body(step, carry):
             getattr(make(step), method)()
             return carry
-        lax.fori_loop(1, count, body, 0, unroll=method != "wait_send")
+        lax.fori_loop(1, count, body, 0)
 
     run(PLANE_PEERS, scatter, "start")
     rs_buf[me] = grams[me]

time: 126 us -> 125 us (level)
  no operation moved by 1% of the time
where the time goes in v8:
time: 125 us
  Pallas kernels  124 us (99%)
    pallas_call x1, Pallas kernels, krylov(): pl.pallas_call(functools.partial(krylov_kernel, z_lo_count, z_hi_count),...  109 us
    pallas_call x1, Pallas kernels, finish(): pl.pallas_call(finish_kernel, out_shape=[jax.ShapeDtypeStruct(right_side....  15 us

profile of v8, /device:TPU:1, one launch (start us, length us, event | category | flops | bytes accessed | tf_op | source)
XLA Modules:
  0.0 124.7 jit_solution(13492708615950127631)
XLA Ops:
  0.6 109.1 %krylov.1 = (f32[32,9,128]{2,1,0:T(8,128)}, f32[4,4,2,3,32,128]{5,4,3,2,1,0:T(8,128)}) custom-call(f32[3,2,2,64,128]{4,3,2,1,0:T(8,128)} %right_hbm.1, f32[3,3,2,128]{3,2,1,0:T(2,128)} %stiff_diag_ref.1, f32[3,3,13,2,128]{4,3,2,1,0:T(2,128)} %stiff_ref.1, f32[3,3,2,128]{3,2,1,0:T(2,128)} %fsai_diag_ref.1, f32[3,3,13,2,128]{4,3,2,1,0:T(2,128)} %fsai_ref.1, ...), custom_call_target="tpu_custom_call" | custom-call | tf_op jit(solution)/shard_map/krylov/pallas_call | solution.py:639
  109.7 15.0 %finish.1 = (f32[3,2,2,64,128]{4,3,2,1,0:T(8,128)}, f32[3,2,2,64,128]{4,3,2,1,0:T(8,128)}) custom-call(f32[32,9,128]{2,1,0:T(8,128)} %get-tuple-element.4.grams_ref, f32[3,2,2,64,128]{4,3,2,1,0:T(8,128)} %right_hbm.1, f32[4,4,2,3,32,128]{5,4,3,2,1,0:T(8,128)} %get-tuple-element.5.basis_hbm), custom_call_target="tpu_custom_call" | custom-call | tf_op jit(solution)/shard_map/finish/pallas_call | solution.py:153
